TPU v7x, 32 devices: a whole 2x2x4 slice. The times are simulated.
32 devices in a mesh: ctx: 16 (over z, y, x), head: 2 (over core).
Axes of the slice: x: 2, y: 2, z: 4, core: 2. Of those that a mesh axis runs over, the one named last changes fastest.
Arguments:
- queries: bfloat16 [8192, 4, 4, 128], P('ctx', 'head')
- keys: bfloat16 [8192, 4, 128], P('ctx')
- values: bfloat16 [8192, 4, 128], P('ctx'), may hold values from -6 to 6
- output_gradient: bfloat16 [8192, 4, 4, 128], P('ctx', 'head'), may hold values from -6 to 6
- selected: int32 [16, 2], replicated, may hold values from 0 to 14, as said below
Outputs:
- attn_out: bfloat16 [8192, 4, 4, 128], P('ctx', 'head')
- grad_q: bfloat16 [8192, 4, 4, 128], P('ctx', 'head')
- grad_k: bfloat16 [8192, 4, 128], P('ctx', 'head')
- grad_v: bfloat16 [8192, 4, 128], P('ctx', 'head')
Inputs may be any that keep to these rules, and one draw needn't show every extreme that they name: selected[b, j] <= b for every block b; an entry equal to b selects no block; for b >= 2 the two entries of a row differ and both are below b.
All inputs are finite; a program needn't handle non-finite values.
Results may differ from a plain program's by a relative error of at most 0.011.
Values may be sent and summed in bfloat16 or wider, within the bound.
A program may use at most 128 MiB of HBM per device.

v0:
```python
import jax
import jax.numpy as jnp
from jax import lax
from jax.sharding import PartitionSpec as P


def fetch_blocks(own_keys, own_values, selected, piece_rows):
    held_keys, held_values = (
        lax.all_to_all(own_keys, "ctx", split_axis=0, concat_axis=0, tiled=True),
        lax.all_to_all(own_values, "ctx", split_axis=0, concat_axis=0, tiled=True),
    )
    blocks = selected.shape[0]
    layout = (blocks, piece_rows) + own_keys.shape[1:]
    wanted = jnp.transpose(selected)
    send_keys = held_keys.reshape(layout)[wanted]
    send_values = held_values.reshape(layout)[wanted]
    got_keys, got_values = (
        lax.all_to_all(send_keys, "ctx", split_axis=1, concat_axis=1, tiled=True),
        lax.all_to_all(send_values, "ctx", split_axis=1, concat_axis=1, tiled=True),
    )
    joined = (2, blocks * piece_rows) + own_keys.shape[1:]
    return (got_keys.reshape(joined), got_values.reshape(joined))


def return_home(part_keys, part_values, selected, piece_rows):
    blocks = selected.shape[0]
    rows_block = blocks * piece_rows
    trailing = part_keys.shape[1:]
    layout = (2, blocks, piece_rows) + trailing
    back_keys, back_values = (
        lax.all_to_all(
            part_keys[: 2 * rows_block].reshape(layout),
            "ctx",
            split_axis=1,
            concat_axis=1,
            tiled=True,
        ),
        lax.all_to_all(
            part_values[: 2 * rows_block].reshape(layout),
            "ctx",
            split_axis=1,
            concat_axis=1,
            tiled=True,
        ),
    )
    owners = (
        jnp.transpose(selected)[:, :, None] == jnp.arange(blocks, dtype=jnp.int32)[None, None, :]
    ).astype(jnp.float32)

    def collect(arrived):
        summed = jnp.einsum(
            "jrb,jrx->bx", owners, arrived.reshape(2, blocks, -1), precision=lax.Precision.HIGHEST
        )
        return summed.reshape((blocks, piece_rows) + trailing)

    home_keys, home_values = (
        lax.all_to_all(collect(back_keys), "ctx", split_axis=0, concat_axis=0, tiled=True),
        lax.all_to_all(collect(back_values), "ctx", split_axis=0, concat_axis=0, tiled=True),
    )
    own_rows = (rows_block,) + trailing
    return (
        home_keys.reshape(own_rows) + part_keys[2 * rows_block :],
        home_values.reshape(own_rows) + part_values[2 * rows_block :],
    )


def attend_head(queries_head, keys_head, values_head, grads_head, visible, softmax_scale):
    scores = (
        jnp.einsum("qgd,kd->gqk", queries_head, keys_head, preferred_element_type=jnp.float32)
        * softmax_scale
    )
    scores = jnp.where(visible[None], scores, -jnp.inf)
    row_max = jnp.max(scores, axis=-1, keepdims=True)
    weights = jnp.exp(scores - row_max)
    probs = weights / jnp.sum(weights, axis=-1, keepdims=True)
    probs_low = probs.astype(jnp.bfloat16)
    head_out = jnp.einsum(
        "gqk,kd->qgd", probs_low, values_head, preferred_element_type=jnp.float32
    ).astype(jnp.bfloat16)
    row_dot = jnp.sum(grads_head.astype(jnp.float32) * head_out.astype(jnp.float32), axis=-1)
    grad_probs = jnp.einsum(
        "qgd,kd->gqk", grads_head, values_head, preferred_element_type=jnp.float32
    )
    grad_scores = (
        probs * (grad_probs - jnp.transpose(row_dot)[:, :, None]) * softmax_scale
    ).astype(jnp.bfloat16)
    head_dq = jnp.einsum(
        "gqk,kd->qgd", grad_scores, keys_head, preferred_element_type=jnp.float32
    ).astype(jnp.bfloat16)
    head_dk = jnp.einsum(
        "gqk,qgd->kd", grad_scores, queries_head, preferred_element_type=jnp.float32
    )
    head_dv = jnp.einsum("gqk,qgd->kd", probs_low, grads_head, preferred_element_type=jnp.float32)
    return (head_out, head_dq, head_dk, head_dv)


def on_device(queries, keys, values, output_gradient, selected):
    rows_block = queries.shape[0]
    kv_count = keys.shape[1]
    head_size = keys.shape[2]
    piece_rows = rows_block // lax.axis_size("ctx")
    own_index = lax.axis_index("ctx")
    softmax_scale = head_size ** (-0.5)
    near_keys, near_values = fetch_blocks(keys, values, selected, piece_rows)
    all_keys = jnp.concatenate([near_keys[0], near_keys[1], keys], axis=0)
    all_values = jnp.concatenate([near_values[0], near_values[1], values], axis=0)
    own_picks = lax.dynamic_index_in_dim(selected, own_index, 0, keepdims=False)
    position = jnp.arange(rows_block, dtype=jnp.int32)
    causal = position[:, None] >= position[None, :]
    visible = jnp.concatenate(
        [
            jnp.broadcast_to(own_picks[0] < own_index, (rows_block, rows_block)),
            jnp.broadcast_to(own_picks[1] < own_index, (rows_block, rows_block)),
            causal,
        ],
        axis=1,
    )

    def per_head(head_pos, totals):
        attn_acc, dq_acc, dk_acc, dv_acc = totals
        head_out, head_dq, head_dk, head_dv = attend_head(
            lax.dynamic_index_in_dim(queries, head_pos, 2, keepdims=False),
            lax.dynamic_index_in_dim(all_keys, head_pos, 1, keepdims=False),
            lax.dynamic_index_in_dim(all_values, head_pos, 1, keepdims=False),
            lax.dynamic_index_in_dim(output_gradient, head_pos, 2, keepdims=False),
            visible,
            softmax_scale,
        )
        attn_acc = lax.dynamic_update_index_in_dim(attn_acc, head_out, head_pos, 2)
        dq_acc = lax.dynamic_update_index_in_dim(dq_acc, head_dq, head_pos, 2)
        dk_acc = lax.dynamic_update_index_in_dim(dk_acc, head_dk, head_pos, 1)
        dv_acc = lax.dynamic_update_index_in_dim(dv_acc, head_dv, head_pos, 1)
        return (attn_acc, dq_acc, dk_acc, dv_acc)

    initial = (
        jnp.zeros(queries.shape, jnp.bfloat16),
        jnp.zeros(queries.shape, jnp.bfloat16),
        jnp.zeros(all_keys.shape, jnp.float32),
        jnp.zeros(all_keys.shape, jnp.float32),
    )
    attn_out, grad_q, part_keys, part_values = lax.fori_loop(0, kv_count, per_head, initial)
    grad_keys, grad_values = return_home(part_keys, part_values, selected, piece_rows)
    grad_keys, grad_values = (
        lax.psum_scatter(grad_keys, "head", scatter_dimension=1, tiled=True),
        lax.psum_scatter(grad_values, "head", scatter_dimension=1, tiled=True),
    )
    return (attn_out, grad_q, grad_keys.astype(jnp.bfloat16), grad_values.astype(jnp.bfloat16))


def solution(mesh):
    return jax.shard_map(
        on_device,
        mesh=mesh,
        in_specs=(
            P("ctx", "head", None, None),
            P("ctx", None, None),
            P("ctx", None, None),
            P("ctx", "head", None, None),
            P(),
        ),
        out_specs=(
            P("ctx", "head", None, None),
            P("ctx", "head", None, None),
            P("ctx", "head", None),
            P("ctx", "head", None),
        ),
        check_vma=False,
    )
```

profile of v0, /device:TPU:0, one launch (start us, length us, event | category | flops | bytes accessed | tf_op | source)
XLA Modules:
  0.0 373.0 jit_solution(18032600717242512195)
XLA Ops:
  7.2 23.4 %all_to_all.40 = bf16[512,4,128]{2,1,0:T(4,128)(2,1)S(1)} all-to-all(bf16[512,4,128]{2,1,0:T(4,128)(2,1)} %param.9), channel_id=1, replica_groups=mesh['ctx'=16,'head'=2] {'ctx'}, dimensions={0} | all-to-all | bytes 1048576 | tf_op jit(solution)/shard_map/all_to_all | solution.py:10
  30.6 3.9 %all-to-all-start.2 = ((bf16[512,4,128]{2,1,0:T(4,128)(2,1)}), bf16[512,4,128]{2,1,0:T(4,128)(2,1)S(1)}, u32[]{:S(2)}, u32[]{:S(2)}) async-start(bf16[512,4,128]{2,1,0:T(4,128)(2,1)} %param.8), calls=%async_computation.2 | async-start | bytes 1048576 | tf_op jit(solution)/shard_map/all_to_all | solution.py:9
  37.3 11.7 %all-to-all-done.2 = bf16[512,4,128]{2,1,0:T(4,128)(2,1)S(1)} async-done(((bf16[512,4,128]{2,1,0:T(4,128)(2,1)}), bf16[512,4,128]{2,1,0:T(4,128)(2,1)S(1)}, u32[]{:S(2)}, u32[]{:S(2)}) %all-to-all-start.2) | async-done | bytes 524320 | tf_op jit(solution)/shard_map/all_to_all | solution.py:9
  49.0 3.9 %all-to-all-start.1 = ((bf16[2,16,32,4,128]{4,2,3,0,1:T(8,128)(2,1)}), bf16[2,16,32,4,128]{4,2,3,0,1:T(8,128)(2,1)S(1)}, u32[]{:S(2)}, u32[]{:S(2)}) async-start(bf16[2,16,32,4,128]{4,2,3,0,1:T(8,128)(2,1)} %copy.141), calls=%async_computation.1 | async-start | bytes 2097152 | tf_op jit(solution)/shard_map/all_to_all | solution.py:19
  54.8 21.7 %all-to-all-done.1 = bf16[2,16,32,4,128]{4,2,3,0,1:T(8,128)(2,1)S(1)} async-done(((bf16[2,16,32,4,128]{4,2,3,0,1:T(8,128)(2,1)}), bf16[2,16,32,4,128]{4,2,3,0,1:T(8,128)(2,1)S(1)}, u32[]{:S(2)}, u32[]{:S(2)}) %all-to-all-start.1) | async-done | bytes 1048608 | tf_op jit(solution)/shard_map/all_to_all | solution.py:19
  76.5 5.9 %all-to-all-start.3 = ((bf16[2,16,32,4,128]{4,2,3,0,1:T(8,128)(2,1)}), bf16[2,16,32,4,128]{4,2,3,0,1:T(8,128)(2,1)S(1)}, u32[]{:S(2)}, u32[]{:S(2)}) async-start(bf16[2,16,32,4,128]{4,2,3,0,1:T(8,128)(2,1)} %copy.147), calls=%async_computation.3 | async-start | bytes 2097152 | tf_op jit(solution)/shard_map/all_to_all | solution.py:18
  86.1 2.3 copy.152
  90.2 2.2 pad_add_fusion
  94.2 11.1 %all-to-all-done.3 = bf16[2,16,32,4,128]{4,2,3,0,1:T(8,128)(2,1)S(1)} async-done(((bf16[2,16,32,4,128]{4,2,3,0,1:T(8,128)(2,1)}), bf16[2,16,32,4,128]{4,2,3,0,1:T(8,128)(2,1)S(1)}, u32[]{:S(2)}, u32[]{:S(2)}) %all-to-all-start.3) | async-done | bytes 1048608 | tf_op jit(solution)/shard_map/all_to_all | solution.py:18
  106.5 2.4 pad_maximum_fusion
  108.9 75.0 %while.19 = (s32[]{:T(128)}, bf16[512,2,4,128]{0,3,1,2:T(8,128)(2,1)}, bf16[512,2,4,128]{0,3,1,2:T(8,128)(2,1)}, f32[1536,4,128]{2,0,1:T(8,128)}, f32[1536,4,128...) while((s32[]{:T(128)}, ...), condition=%wide.region_4.5_spmd, body=%wide.region_0.4_spmd.sunk | while | flops 2434007552 | bytes 79718664 | solution.py:141
  108.9 6.1 %fusion.107 = (f32[2,512]{1,0:T(2,128)S(1)}, f32[2,512,1536]{1,2,0:T(8,128)}) fusion(pred[512,1536]{0,1:T(8,128)(4,1)S(1)} %get-tuple-element.393, bf16[1536,4,128]{2,0,1:T(8,128)(2,1)} %get-tuple-element.394, s32[]{:T(128)} %get-tuple-element.376, bf16[512,2,4,128]{3,0,1,2:T(8,128)(2,1)} %get-tuple-element.395), kind=kOutput, calls=%fused_computation.78.clone.1 | convolution fusion | flops 408946176 | bytes 7738368 | tf_op jit(solution)/shard_map/while/body/eval_jaxpr/sub | solution.py:74
  115.1 3.9 %fusion.108 = bf16[2,512,1536]{1,2,0:T(8,128)(2,1)S(1)} fusion(f32[2,512,1536]{1,2,0:T(8,128)} %get-tuple-element.361, f32[2,512]{1,0:T(2,128)S(1)} %get-tuple-element.362), kind=kLoop, calls=%fused_computation.14.clone.1 | loop fusion | flops 3145728 | bytes 9441280 | tf_op jit(solution)/shard_map/while/body/eval_jaxpr/convert_element_type | solution.py:76
  121.2 2.9 fusion.111
  125.8 1.9 fusion.112
  127.6 6.1 %fusion.107 = (f32[2,512]{1,0:T(2,128)S(1)}, f32[2,512,1536]{1,2,0:T(8,128)}) fusion(pred[512,1536]{0,1:T(8,128)(4,1)S(1)} %get-tuple-element.393, bf16[1536,4,128]{2,0,1:T(8,128)(2,1)} %get-tuple-element.394, s32[]{:T(128)} %get-tuple-element.376, bf16[512,2,4,128]{3,0,1,2:T(8,128)(2,1)} %get-tuple-element.395), kind=kOutput, calls=%fused_computation.78.clone.1 | convolution fusion | flops 408946176 | bytes 7738368 | tf_op jit(solution)/shard_map/while/body/eval_jaxpr/sub | solution.py:74
  133.8 3.9 %fusion.108 = bf16[2,512,1536]{1,2,0:T(8,128)(2,1)S(1)} fusion(f32[2,512,1536]{1,2,0:T(8,128)} %get-tuple-element.361, f32[2,512]{1,0:T(2,128)S(1)} %get-tuple-element.362), kind=kLoop, calls=%fused_computation.14.clone.1 | loop fusion | flops 3145728 | bytes 9441280 | tf_op jit(solution)/shard_map/while/body/eval_jaxpr/convert_element_type | solution.py:76
  139.9 2.9 fusion.111
  144.5 1.9 fusion.112
  146.4 6.1 %fusion.107 = (f32[2,512]{1,0:T(2,128)S(1)}, f32[2,512,1536]{1,2,0:T(8,128)}) fusion(pred[512,1536]{0,1:T(8,128)(4,1)S(1)} %get-tuple-element.393, bf16[1536,4,128]{2,0,1:T(8,128)(2,1)} %get-tuple-element.394, s32[]{:T(128)} %get-tuple-element.376, bf16[512,2,4,128]{3,0,1,2:T(8,128)(2,1)} %get-tuple-element.395), kind=kOutput, calls=%fused_computation.78.clone.1 | convolution fusion | flops 408946176 | bytes 7738368 | tf_op jit(solution)/shard_map/while/body/eval_jaxpr/sub | solution.py:74
  152.5 3.9 %fusion.108 = bf16[2,512,1536]{1,2,0:T(8,128)(2,1)S(1)} fusion(f32[2,512,1536]{1,2,0:T(8,128)} %get-tuple-element.361, f32[2,512]{1,0:T(2,128)S(1)} %get-tuple-element.362), kind=kLoop, calls=%fused_computation.14.clone.1 | loop fusion | flops 3145728 | bytes 9441280 | tf_op jit(solution)/shard_map/while/body/eval_jaxpr/convert_element_type | solution.py:76
  158.7 3.0 fusion.111
  163.3 1.9 fusion.112
  165.1 6.1 %fusion.107 = (f32[2,512]{1,0:T(2,128)S(1)}, f32[2,512,1536]{1,2,0:T(8,128)}) fusion(pred[512,1536]{0,1:T(8,128)(4,1)S(1)} %get-tuple-element.393, bf16[1536,4,128]{2,0,1:T(8,128)(2,1)} %get-tuple-element.394, s32[]{:T(128)} %get-tuple-element.376, bf16[512,2,4,128]{3,0,1,2:T(8,128)(2,1)} %get-tuple-element.395), kind=kOutput, calls=%fused_computation.78.clone.1 | convolution fusion | flops 408946176 | bytes 7738368 | tf_op jit(solution)/shard_map/while/body/eval_jaxpr/sub | solution.py:74
  171.3 3.9 %fusion.108 = bf16[2,512,1536]{1,2,0:T(8,128)(2,1)S(1)} fusion(f32[2,512,1536]{1,2,0:T(8,128)} %get-tuple-element.361, f32[2,512]{1,0:T(2,128)S(1)} %get-tuple-element.362), kind=kLoop, calls=%fused_computation.14.clone.1 | loop fusion | flops 3145728 | bytes 9441280 | tf_op jit(solution)/shard_map/while/body/eval_jaxpr/convert_element_type | solution.py:76
  177.5 2.9 fusion.111
  182.0 1.9 fusion.112
  185.6 3.1 copy.159
  188.7 6.0 %all-to-all-start.6 = ((f32[2,16,32,4,128]{4,3,2,0,1:T(4,128)}), f32[2,16,32,4,128]{4,3,2,0,1:T(4,128)S(1)}, u32[]{:S(2)}, u32[]{:S(2)}) async-start(f32[2,16,32,4,128]{4,3,2,0,1:T(4,128)} %copy.159), calls=%async_computation.7 | async-start | bytes 4194304 | tf_op jit(solution)/shard_map/all_to_all | solution.py:38
  196.5 3.1 copy.154
  199.6 36.9 %all-to-all-done.6 = f32[2,16,32,4,128]{4,3,2,0,1:T(4,128)S(1)} async-done(((f32[2,16,32,4,128]{4,3,2,0,1:T(4,128)}), f32[2,16,32,4,128]{4,3,2,0,1:T(4,128)S(1)}, u32[]{:S(2)}, u32[]{:S(2)}) %all-to-all-start.6) | async-done | bytes 2097184 | tf_op jit(solution)/shard_map/all_to_all | solution.py:38
  237.9 9.8 %all-to-all-start.4 = ((f32[2,16,32,4,128]{4,3,2,0,1:T(4,128)}), f32[2,16,32,4,128]{4,3,2,0,1:T(4,128)S(1)}, u32[]{:S(2)}, u32[]{:S(2)}) async-start(f32[2,16,32,4,128]{4,3,2,0,1:T(4,128)} %copy.154), calls=%async_computation.4 | async-start | bytes 4194304 | tf_op jit(solution)/shard_map/all_to_all | solution.py:31
  247.7 3.9 %reshape.93 = f32[2,16,16384]{2,0,1:T(2,128)} reshape(f32[2,16,32,4,128]{4,3,2,0,1:T(4,128)} %copy-done) | data formatting | bytes 4194304 | tf_op jit(solution)/shard_map/reshape | solution.py:52
  251.6 4.2 %copy.200 = f32[2,16,16384]{2,1,0:T(8,128)} copy(f32[2,16,16384]{2,0,1:T(2,128)} %reshape.93) | data formatting | bytes 4194304 | tf_op jit(solution)/shard_map/reshape | solution.py:52
  255.7 3.6 dot_general.60
  259.4 3.5 fusion.59
  264.3 25.9 %all-to-all-done.4 = f32[2,16,32,4,128]{4,3,2,0,1:T(4,128)S(1)} async-done(((f32[2,16,32,4,128]{4,3,2,0,1:T(4,128)}), f32[2,16,32,4,128]{4,3,2,0,1:T(4,128)S(1)}, u32[]{:S(2)}, u32[]{:S(2)}) %all-to-all-start.4) | async-done | bytes 2097184 | tf_op jit(solution)/shard_map/all_to_all | solution.py:31
  290.2 9.8 %all-to-all-start.7 = ((f32[16,32,4,128]{3,2,1,0:T(4,128)}), f32[16,32,4,128]{3,2,1,0:T(4,128)S(1)}, u32[]{:S(2)}, u32[]{:S(2)}) async-start(f32[16,32,4,128]{3,2,1,0:T(4,128)} %copy.162), calls=%async_computation.8 | async-start | bytes 2097152 | tf_op jit(solution)/shard_map/all_to_all | solution.py:58
  300.0 2.7 reshape.92
  302.7 2.8 copy.201
  305.5 2.4 dot_general.57
  307.9 3.5 fusion.56
  312.8 10.9 %all-to-all-done.7 = f32[16,32,4,128]{3,2,1,0:T(4,128)S(1)} async-done(((f32[16,32,4,128]{3,2,1,0:T(4,128)}), f32[16,32,4,128]{3,2,1,0:T(4,128)S(1)}, u32[]{:S(2)}, u32[]{:S(2)}) %all-to-all-start.7) | async-done | bytes 1048608 | tf_op jit(solution)/shard_map/all_to_all | solution.py:58
  323.7 5.9 %all-to-all-start.5 = ((f32[16,32,4,128]{3,2,1,0:T(4,128)}), f32[16,32,4,128]{3,2,1,0:T(4,128)S(1)}, u32[]{:S(2)}, u32[]{:S(2)}) async-start(f32[16,32,4,128]{3,2,1,0:T(4,128)} %copy.157), calls=%async_computation.5 | async-start | bytes 2097152 | tf_op jit(solution)/shard_map/all_to_all | solution.py:57
  329.7 2.4 bitcast_add_fusion
  332.2 20.3 %all-to-all-done.5 = f32[16,32,4,128]{3,2,1,0:T(4,128)S(1)} async-done(((f32[16,32,4,128]{3,2,1,0:T(4,128)}), f32[16,32,4,128]{3,2,1,0:T(4,128)S(1)}, u32[]{:S(2)}, u32[]{:S(2)}) %all-to-all-start.5) | async-done | bytes 1048608 | tf_op jit(solution)/shard_map/all_to_all | solution.py:57
  352.7 2.4 bitcast_add_fusion.1
  360.1 3.9 %reduce-scatter.3.cloned.1.call-done = f32[512,2,128]{2,0,1:T(8,128)} async-done(((f32[512,4,128]{2,0,1:T(8,128)}), f32[512,2,128]{2,0,1:T(8,128)}) %reduce-scatter.3.cloned.1.call-update) | async-done | bytes 524304 | tf_op jit(solution)/shard_map/reduce_scatter | solution.py:144
  (131 shorter events, 42.2 us)
Async XLA Ops:
  30.6 18.4 %all-to-all-start.2 = ((bf16[512,4,128]{2,1,0:T(4,128)(2,1)}), bf16[512,4,128]{2,1,0:T(4,128)(2,1)S(1)}, u32[]{:S(2)}, u32[]{:S(2)}) async-start(bf16[512,4,128]{2,1,0:T(4,128)(2,1)} %param.8), calls=%async_computation.2 | async-start | bytes 1048576 | tf_op jit(solution)/shard_map/all_to_all | solution.py:9
  49.0 27.5 %all-to-all-start.1 = ((bf16[2,16,32,4,128]{4,2,3,0,1:T(8,128)(2,1)}), bf16[2,16,32,4,128]{4,2,3,0,1:T(8,128)(2,1)S(1)}, u32[]{:S(2)}, u32[]{:S(2)}) async-start(bf16[2,16,32,4,128]{4,2,3,0,1:T(8,128)(2,1)} %copy.141), calls=%async_computation.1 | async-start | bytes 2097152 | tf_op jit(solution)/shard_map/all_to_all | solution.py:19
  53.0 29.4 %copy-start.3 = (bf16[512,4,128]{2,1,0:T(4,128)(2,1)S(1)}, bf16[512,4,128]{2,1,0:T(4,128)(2,1)}, u32[]{:S(2)}) copy-start(bf16[512,4,128]{2,1,0:T(4,128)(2,1)} %param.9) | copy-start | bytes 1572868
  53.8 29.5 %copy-start.4 = (bf16[512,4,128]{2,1,0:T(4,128)(2,1)S(1)}, bf16[512,4,128]{2,1,0:T(4,128)(2,1)}, u32[]{:S(2)}) copy-start(bf16[512,4,128]{2,1,0:T(4,128)(2,1)} %param.8) | copy-start | bytes 1572868
  53.8 30.4 %copy-start.12 = (s32[16,2]{0,1:T(2,128)S(1)}, s32[16,2]{0,1:T(2,128)}, u32[]{:S(2)}) copy-start(s32[16,2]{0,1:T(2,128)} %param.11) | copy-start | bytes 388
  76.5 28.8 %all-to-all-start.3 = ((bf16[2,16,32,4,128]{4,2,3,0,1:T(8,128)(2,1)}), bf16[2,16,32,4,128]{4,2,3,0,1:T(8,128)(2,1)S(1)}, u32[]{:S(2)}, u32[]{:S(2)}) async-start(bf16[2,16,32,4,128]{4,2,3,0,1:T(8,128)(2,1)} %copy.147), calls=%async_computation.3 | async-start | bytes 2097152 | tf_op jit(solution)/shard_map/all_to_all | solution.py:18
  105.3 1.0 copy-start.1
  105.3 1.2 copy-start.2
  106.5 2.4 copy-start.11
  115.0 4.6 %slice-start = ((s8[6291456]{0:T(1024)(128)(4,1)}), s8[4194304]{0:T(1024)(128)(4,1)S(1)}, s32[]{:S(2)}) async-start(s8[6291456]{0:T(1024)(128)(4,1)} %bitcast.170), calls=%async_computation.12 | async-start | bytes 8388608 | tf_op jit(solution)/shard_map/while
  115.0 3.9 %copy-start.5 = (bf16[512,2,4,128]{0,3,1,2:T(8,128)(2,1)S(1)}, bf16[512,2,4,128]{0,3,1,2:T(8,128)(2,1)}, u32[]{:S(2)}) copy-start(bf16[512,2,4,128]{0,3,1,2:T(8,128)(2,1)} %get-tuple-element.377) | copy-start | bytes 3145732 | tf_op jit(solution)/shard_map/while
  115.0 5.0 %slice-start.1 = ((s8[6291456]{0:T(1024)(128)(4,1)}), s8[2097152]{0:T(1024)(128)(4,1)S(1)}, s32[]{:S(2)}) async-start(s8[6291456]{0:T(1024)(128)(4,1)} %bitcast.170), calls=%async_computation.13 | async-start | bytes 4194304 | tf_op jit(solution)/shard_map/while
  119.6 1.6 copy-start.6
  121.2 2.9 copy-start.8
  125.8 1.9 copy-start.9
  133.8 4.6 %slice-start = ((s8[6291456]{0:T(1024)(128)(4,1)}), s8[4194304]{0:T(1024)(128)(4,1)S(1)}, s32[]{:S(2)}) async-start(s8[6291456]{0:T(1024)(128)(4,1)} %bitcast.170), calls=%async_computation.12 | async-start | bytes 8388608 | tf_op jit(solution)/shard_map/while
  133.8 3.9 %copy-start.5 = (bf16[512,2,4,128]{0,3,1,2:T(8,128)(2,1)S(1)}, bf16[512,2,4,128]{0,3,1,2:T(8,128)(2,1)}, u32[]{:S(2)}) copy-start(bf16[512,2,4,128]{0,3,1,2:T(8,128)(2,1)} %get-tuple-element.377) | copy-start | bytes 3145732 | tf_op jit(solution)/shard_map/while
  133.8 5.0 %slice-start.1 = ((s8[6291456]{0:T(1024)(128)(4,1)}), s8[2097152]{0:T(1024)(128)(4,1)S(1)}, s32[]{:S(2)}) async-start(s8[6291456]{0:T(1024)(128)(4,1)} %bitcast.170), calls=%async_computation.13 | async-start | bytes 4194304 | tf_op jit(solution)/shard_map/while
  138.3 1.7 copy-start.6
  139.9 2.9 copy-start.8
  144.5 1.9 copy-start.9
  152.5 4.6 %slice-start = ((s8[6291456]{0:T(1024)(128)(4,1)}), s8[4194304]{0:T(1024)(128)(4,1)S(1)}, s32[]{:S(2)}) async-start(s8[6291456]{0:T(1024)(128)(4,1)} %bitcast.170), calls=%async_computation.12 | async-start | bytes 8388608 | tf_op jit(solution)/shard_map/while
  152.5 3.9 %copy-start.5 = (bf16[512,2,4,128]{0,3,1,2:T(8,128)(2,1)S(1)}, bf16[512,2,4,128]{0,3,1,2:T(8,128)(2,1)}, u32[]{:S(2)}) copy-start(bf16[512,2,4,128]{0,3,1,2:T(8,128)(2,1)} %get-tuple-element.377) | copy-start | bytes 3145732 | tf_op jit(solution)/shard_map/while
  152.5 5.0 %slice-start.1 = ((s8[6291456]{0:T(1024)(128)(4,1)}), s8[2097152]{0:T(1024)(128)(4,1)S(1)}, s32[]{:S(2)}) async-start(s8[6291456]{0:T(1024)(128)(4,1)} %bitcast.170), calls=%async_computation.13 | async-start | bytes 4194304 | tf_op jit(solution)/shard_map/while
  157.0 1.7 copy-start.6
  158.7 3.0 copy-start.8
  163.3 1.9 copy-start.9
  171.3 4.6 %slice-start = ((s8[6291456]{0:T(1024)(128)(4,1)}), s8[4194304]{0:T(1024)(128)(4,1)S(1)}, s32[]{:S(2)}) async-start(s8[6291456]{0:T(1024)(128)(4,1)} %bitcast.170), calls=%async_computation.12 | async-start | bytes 8388608 | tf_op jit(solution)/shard_map/while
  171.3 3.9 %copy-start.5 = (bf16[512,2,4,128]{0,3,1,2:T(8,128)(2,1)S(1)}, bf16[512,2,4,128]{0,3,1,2:T(8,128)(2,1)}, u32[]{:S(2)}) copy-start(bf16[512,2,4,128]{0,3,1,2:T(8,128)(2,1)} %get-tuple-element.377) | copy-start | bytes 3145732 | tf_op jit(solution)/shard_map/while
  171.3 5.0 %slice-start.1 = ((s8[6291456]{0:T(1024)(128)(4,1)}), s8[2097152]{0:T(1024)(128)(4,1)S(1)}, s32[]{:S(2)}) async-start(s8[6291456]{0:T(1024)(128)(4,1)} %bitcast.170), calls=%async_computation.13 | async-start | bytes 4194304 | tf_op jit(solution)/shard_map/while
  175.8 1.7 copy-start.6
  177.5 2.9 copy-start.8
  182.0 1.9 copy-start.9
  188.7 47.8 %all-to-all-start.6 = ((f32[2,16,32,4,128]{4,3,2,0,1:T(4,128)}), f32[2,16,32,4,128]{4,3,2,0,1:T(4,128)S(1)}, u32[]{:S(2)}, u32[]{:S(2)}) async-start(f32[2,16,32,4,128]{4,3,2,0,1:T(4,128)} %copy.159), calls=%async_computation.7 | async-start | bytes 4194304 | tf_op jit(solution)/shard_map/all_to_all | solution.py:38
  236.5 1.4 copy-start
  237.9 52.3 %all-to-all-start.4 = ((f32[2,16,32,4,128]{4,3,2,0,1:T(4,128)}), f32[2,16,32,4,128]{4,3,2,0,1:T(4,128)S(1)}, u32[]{:S(2)}, u32[]{:S(2)}) async-start(f32[2,16,32,4,128]{4,3,2,0,1:T(4,128)} %copy.154), calls=%async_computation.4 | async-start | bytes 4194304 | tf_op jit(solution)/shard_map/all_to_all | solution.py:31
  290.2 33.5 %all-to-all-start.7 = ((f32[16,32,4,128]{3,2,1,0:T(4,128)}), f32[16,32,4,128]{3,2,1,0:T(4,128)S(1)}, u32[]{:S(2)}, u32[]{:S(2)}) async-start(f32[16,32,4,128]{3,2,1,0:T(4,128)} %copy.162), calls=%async_computation.8 | async-start | bytes 2097152 | tf_op jit(solution)/shard_map/all_to_all | solution.py:58
  323.7 28.8 %all-to-all-start.5 = ((f32[16,32,4,128]{3,2,1,0:T(4,128)}), f32[16,32,4,128]{3,2,1,0:T(4,128)S(1)}, u32[]{:S(2)}, u32[]{:S(2)}) async-start(f32[16,32,4,128]{3,2,1,0:T(4,128)} %copy.157), calls=%async_computation.5 | async-start | bytes 2097152 | tf_op jit(solution)/shard_map/all_to_all | solution.py:57
  329.5 28.5 %reduce-scatter.5.cloned.1.call-start = ((), (), s32[]{:S(2)}) async-start(), calls=%async_computation.11 | async-start | bytes 1572864 | tf_op jit(solution)/shard_map/reduce_scatter | solution.py:145
  332.2 23.0 %copy-start.7 = (bf16[512,2,4,128]{0,3,1,2:T(8,128)(2,1)S(1)}, bf16[512,2,4,128]{0,3,1,2:T(8,128)(2,1)}, u32[]{:S(2)}) copy-start(bf16[512,2,4,128]{0,3,1,2:T(8,128)(2,1)} %get-tuple-element.260) | copy-start | bytes 3145732
  332.2 31.9 %reduce-scatter.3.cloned.1.call-start = ((), (), s32[]{:S(2)}) async-start(), calls=%async_computation.10 | async-start | bytes 1572864 | tf_op jit(solution)/shard_map/reduce_scatter | solution.py:144
  352.7 4.0 %copy-start.10 = (bf16[512,2,4,128]{0,3,1,2:T(8,128)(2,1)S(1)}, bf16[512,2,4,128]{0,3,1,2:T(8,128)(2,1)}, u32[]{:S(2)}) copy-start(bf16[512,2,4,128]{0,3,1,2:T(8,128)(2,1)} %get-tuple-element.261) | copy-start | bytes 3145732
Sparse Core Ops, SparseCore 0:
  332.6 9.6 reduce-scatter.4
  355.2 8.7 reduce-scatter.2
where the time goes:
time: 375 us; the launch traced here: 373 us
  waiting for transfers between devices  142 us (38%)
  matrix products  64.4 us (17%)
  local copies, waits for them, and re-layouts  53.3 us (14%)
  starting transfers between devices  45.3 us (12%)
  other arithmetic  28.3 us (8%)
  blocking collectives  23.4 us (6%)
  between operations  15.6 us (4%)
    all_to_all x1, waiting for transfers between devices, return_home(): lax.all_to_all(part_values[:2 * rows_block].reshape(layout), 'ctx', split...  36.9 us
    all_to_all x1, waiting for transfers between devices, return_home(): lax.all_to_all(part_keys[:2 * rows_block].reshape(layout), 'ctx', split_a...  25.9 us
    sub x4, matrix products, attend_head(): weights = jnp.exp(scores - row_max)  24.5 us
    all_to_all x1, blocking collectives, fetch_blocks(): lax.all_to_all(own_values, 'ctx', split_axis=0, concat_axis=0, tiled=True)  23.4 us
    all_to_all x1, waiting for transfers between devices, fetch_blocks(): lax.all_to_all(send_values, 'ctx', split_axis=1, concat_axis=1, tiled=True)  21.7 us
    all_to_all x1, waiting for transfers between devices, return_home(): lax.all_to_all(collect(back_keys), 'ctx', split_axis=0, concat_axis=0, ti...  20.3 us
    convert_element_type x4, other arithmetic, attend_head(): probs_low = probs.astype(jnp.bfloat16)  15.5 us
    reshape x4, local copies, waits for them, and re-layouts, collect(): arrived.reshape(2, blocks, -1)  13.6 us
  transfers between devices with their start and end apart: 9, of which 8 were waited for; matrix products, arithmetic and copies ran while one was open for 16% of the time, Pallas kernels for 0%

commit v1 on v0

v1 whole, which is shorter than its diff:
```python
import functools
import math

import jax
import jax.numpy as jnp
from jax import lax
from jax.experimental import pallas as pl
from jax.experimental.pallas import tpu as pltpu
from jax.sharding import PartitionSpec as P

F32 = jnp.float32
BF16 = jnp.bfloat16


def dot_nt(a, b):
    return lax.dot_general(a, b, (((1,), (1,)), ((), ())), preferred_element_type=F32)


def dot_nn(a, b):
    return lax.dot_general(a, b, (((1,), (0,)), ((), ())), preferred_element_type=F32)


def attend_kernel(tile, vis_ref, q_ref, do_ref, near_ref, own_ref, out_ref, dq_ref, dnear_ref,
                  down_ref, kt_ref, vt_ref, dk_ref, dv_ref):
    g = pl.program_id(1)
    rows, size = q_ref.shape[2], q_ref.shape[3]
    scale = size ** -0.5
    factor = scale * math.log2(math.e)

    def keys_of(j):
        return near_ref.at[j, 0, 0] if j < 2 else own_ref.at[0, 0]

    def values_of(j):
        return near_ref.at[j, 1, 0] if j < 2 else own_ref.at[1, 0]

    @pl.when(g == 0)
    def _():
        for j in range(3):
            kt_ref[:, j * rows:(j + 1) * rows] = keys_of(j)[...].astype(F32).T.astype(BF16)
            vt_ref[:, j * rows:(j + 1) * rows] = values_of(j)[...].astype(F32).T.astype(BF16)
        dk_ref[...] = jnp.zeros_like(dk_ref)
        dv_ref[...] = jnp.zeros_like(dv_ref)

    for t in range(rows // tile):
        span = slice(t * tile, (t + 1) * tile)
        q = q_ref[0, 0, span, :]
        do = do_ref[0, 0, span, :]
        do_t = do.astype(F32).T
        do_tb = do_t.astype(BF16)
        q_tb = q.astype(F32).T.astype(BF16)
        counts = (rows, rows, (t + 1) * tile)
        scores, tops = [], []
        for j in range(3):
            s = dot_nn(keys_of(j)[0:counts[j], :], q_tb) * factor
            if j == 2:
                key_at = lax.broadcasted_iota(jnp.int32, s.shape, 0)
                query_at = lax.broadcasted_iota(jnp.int32, s.shape, 1) + t * tile
                s = jnp.where(key_at <= query_at, s, -jnp.inf)
            top = jnp.max(s, axis=0, keepdims=True)
            if j < 2:
                top = jnp.where(vis_ref[j] > 0, top, -jnp.inf)
            scores.append(s)
            tops.append(top)
        top = jnp.maximum(jnp.maximum(tops[0], tops[1]), tops[2])
        total = jnp.zeros_like(top)
        weights = []
        for j in range(3):
            shift = jnp.where(vis_ref[j] > 0, top, jnp.inf) if j < 2 else top
            e = jnp.exp2(scores[j] - shift)
            total = total + jnp.sum(e, axis=0, keepdims=True)
            weights.append(e)
        inverse = 1.0 / total
        out_t = jnp.zeros((size, tile), F32)
        lows, probs = [], []
        for j in range(3):
            p = weights[j] * inverse
            low = p.astype(BF16)
            probs.append(p)
            lows.append(low)
            out_t = out_t + dot_nn(vt_ref[:, j * rows:j * rows + counts[j]], low)
        out_low = out_t.astype(BF16).astype(F32)
        out_ref[0, 0, span, :] = out_low.T.astype(BF16)
        row_dot = jnp.sum(do_t * out_low, axis=0, keepdims=True)
        dq_t = jnp.zeros((size, tile), F32)
        for j in range(3):
            dp = dot_nn(values_of(j)[0:counts[j], :], do_tb)
            ds = (probs[j] * (dp - row_dot)).astype(BF16)
            dq_t = dq_t + dot_nn(kt_ref[:, j * rows:j * rows + counts[j]], ds)
            dk_ref[j, 0:counts[j], :] += dot_nn(ds, q)
            dv_ref[j, 0:counts[j], :] += dot_nn(lows[j], do)
        dq_ref[0, 0, span, :] = (dq_t * scale).T.astype(BF16)

    @pl.when(g == pl.num_programs(1) - 1)
    def _():
        for j in range(2):
            dnear_ref[j, 0, 0] = (dk_ref[j] * scale).astype(BF16)
            dnear_ref[j, 1, 0] = dv_ref[j].astype(BF16)
        down_ref[0, 0] = dk_ref[2] * scale
        down_ref[1, 0] = dv_ref[2]


def attend(visible, q, do, near, own):
    heads, group, rows, size = q.shape
    tile = min(256, rows)
    head_spec = pl.BlockSpec((1, 1, rows, size), lambda n, g, *_: (n, g, 0, 0))
    near_spec = pl.BlockSpec((2, 2, 1, rows, size), lambda n, g, *_: (0, 0, n, 0, 0))
    own_spec = pl.BlockSpec((2, 1, rows, size), lambda n, g, *_: (0, n, 0, 0))
    return pl.pallas_call(
        functools.partial(attend_kernel, tile),
        grid_spec=pltpu.PrefetchScalarGridSpec(
            num_scalar_prefetch=1,
            grid=(heads, group),
            in_specs=[head_spec, head_spec, near_spec, own_spec],
            out_specs=[head_spec, head_spec, near_spec, own_spec],
            scratch_shapes=[
                pltpu.VMEM((size, 3 * rows), BF16),
                pltpu.VMEM((size, 3 * rows), BF16),
                pltpu.VMEM((3, rows, size), F32),
                pltpu.VMEM((3, rows, size), F32),
            ],
        ),
        out_shape=[
            jax.ShapeDtypeStruct(q.shape, BF16),
            jax.ShapeDtypeStruct(q.shape, BF16),
            jax.ShapeDtypeStruct(near.shape, BF16),
            jax.ShapeDtypeStruct(own.shape, F32),
        ],
        compiler_params=pltpu.CompilerParams(vmem_limit_bytes=56 * 2**20),
    )(visible, q, do, near, own)


def on_device(queries, keys, values, output_gradient, selected):
    rows, kv_count, size = keys.shape
    blocks = lax.axis_size("ctx")
    own_heads = kv_count // lax.axis_size("head")
    me = lax.axis_index("ctx")
    half = lax.axis_index("head")

    def to_heads(x):
        x = lax.all_to_all(x, "head", split_axis=2, concat_axis=1, tiled=True)
        return jnp.transpose(x, (2, 1, 0, 3))

    def from_heads(x):
        x = jnp.transpose(x, (2, 1, 0, 3))
        return lax.all_to_all(x, "head", split_axis=1, concat_axis=2, tiled=True)

    q, do = to_heads(queries), to_heads(output_gradient)
    own = jnp.stack([keys, values])
    own = lax.dynamic_slice_in_dim(own, half * own_heads, own_heads, 2)
    own = jnp.transpose(own, (0, 2, 1, 3))
    piece = 2 * own_heads * rows // blocks
    flat = own.reshape(blocks, piece, size)
    held = lax.all_to_all(flat, "ctx", split_axis=0, concat_axis=0, tiled=True)
    near = lax.all_to_all(held[jnp.transpose(selected)], "ctx", split_axis=1, concat_axis=1, tiled=True)
    near = near.reshape((2,) + own.shape)
    visible = (lax.dynamic_index_in_dim(selected, me, 0, keepdims=False) < me).astype(jnp.int32)
    out, dq, dnear, down = attend(visible, q, do, near, own)
    back = lax.all_to_all(dnear.reshape(2, blocks, piece, size), "ctx", split_axis=1, concat_axis=1, tiled=True)
    owners = (jnp.transpose(selected)[:, :, None] == jnp.arange(blocks, dtype=jnp.int32)).astype(BF16)
    home = jnp.einsum("jrb,jrpd->bpd", owners, back, preferred_element_type=F32).astype(BF16)
    home = lax.all_to_all(home, "ctx", split_axis=0, concat_axis=0, tiled=True)
    grads = (home.reshape(own.shape).astype(F32) + down).astype(BF16)
    grads = jnp.transpose(grads, (0, 2, 1, 3))
    return from_heads(out), from_heads(dq), grads[0], grads[1]


def solution(mesh):
    return jax.shard_map(
        on_device,
        mesh=mesh,
        in_specs=(
            P("ctx", "head", None, None),
            P("ctx", None, None),
            P("ctx", None, None),
            P("ctx", "head", None, None),
            P(),
        ),
        out_specs=(
            P("ctx", "head", None, None),
            P("ctx", "head", None, None),
            P("ctx", "head", None),
            P("ctx", "head", None),
        ),
        check_vma=False,
    )
```

time: 375 us -> 171 us (0.46)
  waiting for transfers between devices: 142 us -> 65.4 us
  matrix products: 64.4 us -> 0.69 us
  Pallas kernels: 0 us -> 34.9 us
  local copies, waits for them, and re-layouts: 53.3 us -> 24.4 us
  other arithmetic: 28.3 us -> 2.52 us
  between operations: 15.6 us -> 0.78 us
  starting transfers between devices: 45.3 us -> 31.7 us
  blocking collectives: 23.4 us -> 9.94 us
    all_to_all x7 -> x6, waiting for transfers between devices: 138 us -> 65.4 us  [the longest x1 21 us: on_device(): lax.all_to_all(dnear.reshape(2, blocks, piece, size), 'ctx', split_axis=1...]
    dot_general x22 -> x1, matrix products: 39.9 us -> 0.69 us  [on_device(): jnp.einsum('jrb,jrpd->bpd', owners, back, preferred_element_type=F32)]
    pallas_call x0 -> x1, Pallas kernels: none -> 34.9 us  [attend(): pl.pallas_call(functools.partial(attend_kernel, tile), grid_spec=pltpu.Pr...]
    sub x4 -> x0, matrix products: 24.5 us -> none  [attend_head(): weights = jnp.exp(scores - row_max)]
    convert_element_type x6 -> x1, other arithmetic: 17.7 us -> 0.7 us  [on_device(): (lax.dynamic_index_in_dim(selected, me, 0, keepdims=False) < me).astype(j...]
    reshape x8 -> x1, local copies, waits for them, and re-layouts: 20 us -> 3.28 us  [on_device(): dnear.reshape(2, blocks, piece, size)]
    all_to_all x1 -> x2, blocking collectives: 23.4 us -> 9.94 us  [the longest x1 5.38 us: to_heads(): x = lax.all_to_all(x, 'head', split_axis=2, concat_axis=1, tiled=True)]
    all_to_all x7 -> x6, starting transfers between devices: 45.2 us -> 31.7 us  [the longest x1 8.47 us: on_device(): held = lax.all_to_all(flat, 'ctx', split_axis=0, concat_axis=0, tiled=True)]
  transfers between devices with their start and end apart: 9 -> 6, of which waited for: 8 -> 5; matrix products, arithmetic and copies ran while one was open for 16% -> 10% of each run, Pallas kernels for 0% -> 0%
where the time goes in v1:
time: 171 us; the launch traced here: 170 us
  waiting for transfers between devices  65.4 us (38%)
  Pallas kernels  34.9 us (20%)
  starting transfers between devices  31.7 us (19%)
  local copies, waits for them, and re-layouts  24.4 us (14%)
  blocking collectives  9.94 us (6%)
  other arithmetic  2.52 us (1%)
    pallas_call x1, Pallas kernels, attend(): pl.pallas_call(functools.partial(attend_kernel, tile), grid_spec=pltpu.Pr...  34.9 us
    all_to_all x1, waiting for transfers between devices, on_device(): lax.all_to_all(dnear.reshape(2, blocks, piece, size), 'ctx', split_axis=1...  21 us
    all_to_all x1, waiting for transfers between devices, on_device(): lax.all_to_all(held[jnp.transpose(selected)], 'ctx', split_axis=1, concat...  20.4 us
    all_to_all x1, waiting for transfers between devices, on_device(): held = lax.all_to_all(flat, 'ctx', split_axis=0, concat_axis=0, tiled=True)  12.3 us
    all_to_all x1, waiting for transfers between devices, on_device(): home = lax.all_to_all(home, 'ctx', split_axis=0, concat_axis=0, tiled=True)  11.3 us
    all_to_all x1, starting transfers between devices, on_device(): held = lax.all_to_all(flat, 'ctx', split_axis=0, concat_axis=0, tiled=True)  8.47 us
    unnamed x20, local copies, waits for them, and re-layouts  6.33 us
    all_to_all x1, starting transfers between devices, on_device(): lax.all_to_all(dnear.reshape(2, blocks, piece, size), 'ctx', split_axis=1...  6.26 us
  transfers between devices with their start and end apart: 6, of which 5 were waited for; matrix products, arithmetic and copies ran while one was open for 10% of the time, Pallas kernels for 0%

profile of v1, /device:TPU:0, one launch (start us, length us, event | category | flops | bytes accessed | tf_op | source)
XLA Modules:
  0.0 170.4 jit_solution(7781826351106042578)
XLA Ops:
  0.6 1.3 copy_bitcast_fusion
  2.0 0.0 copy-start.2
  2.0 0.8 fusion.4
  2.8 8.5 %all-to-all-start.2 = ((bf16[16,128,128]{2,1,0:T(8,128)(2,1)}), bf16[16,128,128]{2,1,0:T(8,128)(2,1)S(1)}, u32[]{:S(2)}, u32[]{:S(2)}) async-start(bf16[16,128,128]{2,1,0:T(8,128)(2,1)} %bitcast.11), calls=%async_computation.2 | async-start | bytes 1048576 | tf_op jit(solution)/shard_map/all_to_all | solution.py:153
  11.3 0.0 copy-done.7
  11.3 0.1 reshape.32
  11.4 0.0 copy-done.2
  11.4 1.1 copy.52
  12.6 0.4 copy-done.3
  13.0 1.1 copy.54
  14.1 12.3 %all-to-all-done.2 = bf16[16,128,128]{2,1,0:T(8,128)(2,1)S(1)} async-done(((bf16[16,128,128]{2,1,0:T(8,128)(2,1)}), bf16[16,128,128]{2,1,0:T(8,128)(2,1)S(1)}, u32[]{:S(2)}, u32[]{:S(2)}) %all-to-all-start.2) | async-done | bytes 524320 | tf_op jit(solution)/shard_map/all_to_all | solution.py:153
  26.4 3.6 %all-to-all-start = ((bf16[512,2,4,128]{3,0,1,2:T(8,128)(2,1)}), bf16[512,2,4,128]{3,0,1,2:T(8,128)(2,1)S(1)}, u32[]{:S(2)}, u32[]{:S(2)}) async-start(bf16[512,2,4,128]{3,0,1,2:T(8,128)(2,1)} %copy.52), calls=%async_computation | async-start | bytes 2097152 | tf_op jit(solution)/shard_map/all_to_all | solution.py:140
  30.0 1.7 gather_fusion
  31.7 2.4 %copy.58 = bf16[2,16,128,128]{3,2,0,1:T(8,128)(2,1)} copy(bf16[2,16,128,128]{3,2,1,0:T(8,128)(2,1)} %bitcast.55) | data formatting | bytes 2097152 | tf_op jit(solution)/shard_map/gather | solution.py:154
  34.1 0.0 all-to-all-done
  34.1 0.0 copy-done
  34.1 5.4 %all_to_all.92 = bf16[512,2,4,128]{3,0,1,2:T(8,128)(2,1)} all-to-all(bf16[512,2,4,128]{3,0,1,2:T(8,128)(2,1)S(1)} %copy-done), channel_id=1, replica_groups=mesh['ctx'=16,'head'=2] {'head'}, dimensions={2} | all-to-all | bytes 2097152 | tf_op jit(solution)/shard_map/all_to_all | solution.py:140
  39.5 3.9 %all-to-all-start.3 = ((bf16[2,16,128,128]{3,2,0,1:T(8,128)(2,1)}), bf16[2,16,128,128]{3,2,0,1:T(8,128)(2,1)S(1)}, u32[]{:S(2)}, u32[]{:S(2)}) async-start(bf16[2,16,128,128]{3,2,0,1:T(8,128)(2,1)} %copy.58), calls=%async_computation.3 | async-start | bytes 2097152 | tf_op jit(solution)/shard_map/all_to_all | solution.py:154
  43.4 0.0 copy-start.1
  43.4 1.0 copy.53
  44.5 0.6 copy-done.1
  45.0 1.0 copy.55
  46.1 0.7 fusion.8.vis_ref
  46.8 0.9 fusion.9.own_ref
  47.6 20.4 %all-to-all-done.3 = bf16[2,16,128,128]{3,2,0,1:T(8,128)(2,1)S(1)} async-done(((bf16[2,16,128,128]{3,2,0,1:T(8,128)(2,1)}), bf16[2,16,128,128]{3,2,0,1:T(8,128)(2,1)S(1)}, u32[]{:S(2)}, u32[]{:S(2)}) %all-to-all-start.3) | async-done | bytes 1048608 | tf_op jit(solution)/shard_map/all_to_all | solution.py:154
  68.0 1.1 copy.59
  69.1 34.9 %shard_map.84 = (bf16[2,4,512,128]{3,2,1,0:T(8,128)(2,1)}, bf16[2,4,512,128]{3,2,1,0:T(8,128)(2,1)}, bf16[2,2,2,512,128]{4,3,2,1,0:T(8,128)(2,1)}, f32[2,2,512,128]{3,2,1,0:T(8,128)}) custom-call(s32[2]{0:T(128)} %fusion.8.vis_ref, bf16[2,4,512,128]{3,2,1,0:T(8,128)(2,1)} %bitcast.56, bf16[2,4,512,128]{3,2,1,0:T(8,128)(2,1)} %bitcast.57, ...), custom_call_target="tpu_custom_call" | custom-call | tf_op jit(solution)/shard_map/pallas_call | solution.py:108
  104.0 3.3 %copy.64 = bf16[2,16,128,128]{3,0,2,1:T(2,128)(2,1)} copy(bf16[2,16,128,128]{3,2,1,0:T(8,128)(2,1)} %bitcast.64) | data formatting | bytes 2097152 | tf_op jit(solution)/shard_map/reshape | solution.py:158
  107.3 6.3 %all-to-all-start.6 = ((bf16[2,16,128,128]{3,0,2,1:T(2,128)(2,1)}), bf16[2,16,128,128]{3,0,2,1:T(2,128)(2,1)S(1)}, u32[]{:S(2)}, u32[]{:S(2)}) async-start(bf16[2,16,128,128]{3,0,2,1:T(2,128)(2,1)} %copy.64), calls=%async_computation.6 | async-start | bytes 2097152 | tf_op jit(solution)/shard_map/all_to_all | solution.py:158
  113.5 0.0 copy-done.6
  113.6 0.0 copy-start.5
  113.6 0.1 copy.60
  113.6 1.1 copy-done.5
  114.8 1.0 copy.62
  115.8 21.0 %all-to-all-done.6 = bf16[2,16,128,128]{3,0,2,1:T(2,128)(2,1)S(1)} async-done(((bf16[2,16,128,128]{3,0,2,1:T(2,128)(2,1)}), bf16[2,16,128,128]{3,0,2,1:T(2,128)(2,1)S(1)}, u32[]{:S(2)}, u32[]{:S(2)}) %all-to-all-start.6) | async-done | bytes 1048608 | tf_op jit(solution)/shard_map/all_to_all | solution.py:158
  136.8 3.6 %all-to-all-start.5 = ((bf16[512,4,2,128]{3,0,2,1:T(8,128)(2,1)}), bf16[512,4,2,128]{3,0,2,1:T(8,128)(2,1)S(1)}, u32[]{:S(2)}, u32[]{:S(2)}) async-start(bf16[512,4,2,128]{3,0,2,1:T(8,128)(2,1)} %copy.62), calls=%async_computation.5 | async-start | bytes 2097152 | tf_op jit(solution)/shard_map/all_to_all | solution.py:145
  140.4 0.7 fusion
  141.1 1.0 copy.66
  142.0 0.5 all-to-all-done.5
  142.5 4.6 %all_to_all.93 = bf16[512,4,2,128]{3,0,2,1:T(8,128)(2,1)S(1)} all-to-all(bf16[512,4,2,128]{3,0,2,1:T(8,128)(2,1)S(1)} %copy.60), channel_id=1, replica_groups=mesh['ctx'=16,'head'=2] {'head'}, dimensions={1} | all-to-all | bytes 2097152 | tf_op jit(solution)/shard_map/all_to_all | solution.py:145
  147.1 5.9 %all-to-all-start.7 = ((bf16[16,128,128]{2,1,0:T(8,128)(2,1)}), bf16[16,128,128]{2,1,0:T(8,128)(2,1)S(1)}, u32[]{:S(2)}, u32[]{:S(2)}) async-start(bf16[16,128,128]{2,1,0:T(8,128)(2,1)} %copy.66), calls=%async_computation.7 | async-start | bytes 1048576 | tf_op jit(solution)/shard_map/all_to_all | solution.py:161
  152.9 2.0 %copy.63 = bf16[512,2,2,2,128]{4,3,2,1,0:T(2,128)(2,1)} copy(bf16[512,2,2,2,128]{4,0,3,1,2:T(8,128)(2,1)S(1)} %bitcast.53) | data formatting | bytes 2097152 | tf_op jit(solution)/shard_map/all_to_all | solution.py:145
  155.0 2.0 %copy.61 = bf16[512,2,2,2,128]{4,3,2,1,0:T(2,128)(2,1)} copy(bf16[512,2,2,2,128]{4,0,3,1,2:T(8,128)(2,1)S(1)} %bitcast.54) | data formatting | bytes 2097152 | tf_op jit(solution)/shard_map/all_to_all | solution.py:145
  157.0 11.3 %all-to-all-done.7 = bf16[16,128,128]{2,1,0:T(8,128)(2,1)S(1)} async-done(((bf16[16,128,128]{2,1,0:T(8,128)(2,1)}), bf16[16,128,128]{2,1,0:T(8,128)(2,1)S(1)}, u32[]{:S(2)}, u32[]{:S(2)}) %all-to-all-start.7) | async-done | bytes 524320 | tf_op jit(solution)/shard_map/all_to_all | solution.py:161
  168.3 0.0 copy-done.4
  168.3 0.1 fusion.3
  168.5 1.0 copy.68
  169.5 1.0 copy.67
  (8 shorter events, 0.1 us)
Async XLA Ops:
  2.0 9.4 %copy-start.2 = (bf16[512,2,4,128]{3,2,1,0:T(4,128)(2,1)S(1)}, bf16[512,2,4,128]{3,2,1,0:T(4,128)(2,1)}, u32[]{:S(2)}) copy-start(bf16[512,2,4,128]{3,2,1,0:T(4,128)(2,1)} %param.5) | copy-start | bytes 3145732
  2.8 8.5 %copy-start.7 = (s32[16,2]{0,1:T(2,128)S(1)}, s32[16,2]{0,1:T(2,128)}, u32[]{:S(2)}) copy-start(s32[16,2]{0,1:T(2,128)} %param.9) | copy-start | bytes 388
  2.8 23.6 %all-to-all-start.2 = ((bf16[16,128,128]{2,1,0:T(8,128)(2,1)}), bf16[16,128,128]{2,1,0:T(8,128)(2,1)S(1)}, u32[]{:S(2)}, u32[]{:S(2)}) async-start(bf16[16,128,128]{2,1,0:T(8,128)(2,1)} %bitcast.11), calls=%async_computation.2 | async-start | bytes 1048576 | tf_op jit(solution)/shard_map/all_to_all | solution.py:153
  11.4 1.5 copy-start.3
  26.4 7.7 %all-to-all-start = ((bf16[512,2,4,128]{3,0,1,2:T(8,128)(2,1)}), bf16[512,2,4,128]{3,0,1,2:T(8,128)(2,1)S(1)}, u32[]{:S(2)}, u32[]{:S(2)}) async-start(bf16[512,2,4,128]{3,0,1,2:T(8,128)(2,1)} %copy.52), calls=%async_computation | async-start | bytes 2097152 | tf_op jit(solution)/shard_map/all_to_all | solution.py:140
  31.7 2.4 %copy-start = (bf16[512,2,4,128]{3,0,1,2:T(8,128)(2,1)S(1)}, bf16[512,2,4,128]{3,0,1,2:T(8,128)(2,1)}, u32[]{:S(2)}) copy-start(bf16[512,2,4,128]{3,0,1,2:T(8,128)(2,1)} %copy.54) | copy-start | bytes 3145732
  39.5 28.6 %all-to-all-start.3 = ((bf16[2,16,128,128]{3,2,0,1:T(8,128)(2,1)}), bf16[2,16,128,128]{3,2,0,1:T(8,128)(2,1)S(1)}, u32[]{:S(2)}, u32[]{:S(2)}) async-start(bf16[2,16,128,128]{3,2,0,1:T(8,128)(2,1)} %copy.58), calls=%async_computation.3 | async-start | bytes 2097152 | tf_op jit(solution)/shard_map/all_to_all | solution.py:154
  43.4 1.6 copy-start.1
  107.3 6.3 %copy-start.6 = (bf16[2,4,512,128]{3,2,1,0:T(8,128)(2,1)S(1)}, bf16[2,4,512,128]{3,2,1,0:T(8,128)(2,1)}, u32[]{:S(2)}) copy-start(bf16[2,4,512,128]{3,2,1,0:T(8,128)(2,1)} %get-tuple-element.8) | copy-start | bytes 3145732
  107.3 29.5 %all-to-all-start.6 = ((bf16[2,16,128,128]{3,0,2,1:T(2,128)(2,1)}), bf16[2,16,128,128]{3,0,2,1:T(2,128)(2,1)S(1)}, u32[]{:S(2)}, u32[]{:S(2)}) async-start(bf16[2,16,128,128]{3,0,2,1:T(2,128)(2,1)} %copy.64), calls=%async_computation.6 | async-start | bytes 2097152 | tf_op jit(solution)/shard_map/all_to_all | solution.py:158
  113.6 1.2 copy-start.5
  136.8 5.7 %all-to-all-start.5 = ((bf16[512,4,2,128]{3,0,2,1:T(8,128)(2,1)}), bf16[512,4,2,128]{3,0,2,1:T(8,128)(2,1)S(1)}, u32[]{:S(2)}, u32[]{:S(2)}) async-start(bf16[512,4,2,128]{3,0,2,1:T(8,128)(2,1)} %copy.62), calls=%async_computation.5 | async-start | bytes 2097152 | tf_op jit(solution)/shard_map/all_to_all | solution.py:145
  147.1 21.3 %all-to-all-start.7 = ((bf16[16,128,128]{2,1,0:T(8,128)(2,1)}), bf16[16,128,128]{2,1,0:T(8,128)(2,1)S(1)}, u32[]{:S(2)}, u32[]{:S(2)}) async-start(bf16[16,128,128]{2,1,0:T(8,128)(2,1)} %copy.66), calls=%async_computation.7 | async-start | bytes 1048576 | tf_op jit(solution)/shard_map/all_to_all | solution.py:161
  155.0 13.3 %copy-start.4 = (f32[2,2,512,128]{3,2,1,0:T(8,128)S(1)}, f32[2,2,512,128]{3,2,1,0:T(8,128)}, u32[]{:S(2)}) copy-start(f32[2,2,512,128]{3,2,1,0:T(8,128)} %get-tuple-element.11) | copy-start | bytes 3145732

commit v2 on v1

--- a/solution.py
+++ b/solution.py
@@ -28,10 +28,10 @@
     factor = scale * math.log2(math.e)
 
     def keys_of(j):
-        return near_ref.at[j, 0, 0] if j < 2 else own_ref.at[0, 0]
+        return near_ref.at[0, j, 0] if j < 2 else own_ref.at[0, 0]
 
     def values_of(j):
-        return near_ref.at[j, 1, 0] if j < 2 else own_ref.at[1, 0]
+        return near_ref.at[0, j, 1] if j < 2 else own_ref.at[0, 1]
 
     @pl.when(g == 0)
     def _():
@@ -93,18 +93,18 @@
     @pl.when(g == pl.num_programs(1) - 1)
     def _():
         for j in range(2):
-            dnear_ref[j, 0, 0] = (dk_ref[j] * scale).astype(BF16)
-            dnear_ref[j, 1, 0] = dv_ref[j].astype(BF16)
+            dnear_ref[0, j, 0] = (dk_ref[j] * scale).astype(BF16)
+            dnear_ref[0, j, 1] = dv_ref[j].astype(BF16)
         down_ref[0, 0] = dk_ref[2] * scale
-        down_ref[1, 0] = dv_ref[2]
+        down_ref[0, 1] = dv_ref[2]
 
 
 def attend(visible, q, do, near, own):
     heads, group, rows, size = q.shape
     tile = min(256, rows)
     head_spec = pl.BlockSpec((1, 1, rows, size), lambda n, g, *_: (n, g, 0, 0))
-    near_spec = pl.BlockSpec((2, 2, 1, rows, size), lambda n, g, *_: (0, 0, n, 0, 0))
-    own_spec = pl.BlockSpec((2, 1, rows, size), lambda n, g, *_: (0, n, 0, 0))
+    near_spec = pl.BlockSpec((1, 2, 2, rows, size), lambda n, g, *_: (n, 0, 0, 0, 0))
+    own_spec = pl.BlockSpec((1, 2, rows, size), lambda n, g, *_: (n, 0, 0, 0))
     return pl.pallas_call(
         functools.partial(attend_kernel, tile),
         grid_spec=pltpu.PrefetchScalarGridSpec(
@@ -129,39 +129,240 @@
     )(visible, q, do, near, own)
 
 
+def greet(blocks, halves):
+    me, half = lax.axis_index("ctx"), lax.axis_index("head")
+    barrier = pltpu.get_barrier_semaphore()
+
+    @pl.loop(1, blocks)
+    def _(i):
+        pl.semaphore_signal(barrier, inc=1, device_id={"ctx": lax.rem(me + i, blocks), "head": half})
+
+    for i in range(1, halves):
+        pl.semaphore_signal(barrier, inc=1, device_id={"ctx": me, "head": lax.rem(half + i, halves)})
+    pl.semaphore_wait(barrier, blocks - 1 + halves - 1)
+
+
+def fetch_kernel(blocks, halves, sel_ref, kv_ref, q_ref, do_ref, near_ref, qo_ref, doo_ref,
+                 send, stage, s1, r1, s2, r2, local2, xs, xr, xl, *held):
+    me, half = lax.axis_index("ctx"), lax.axis_index("head")
+    heads = kv_ref.shape[0]
+    part = q_ref.shape[1]
+    greet(blocks, halves)
+
+    for n in range(heads):
+        @pl.loop(1, blocks)
+        def _(i):
+            peer = lax.rem(me + i, blocks)
+            pltpu.make_async_remote_copy(
+                kv_ref.at[n, peer], held[n].at[me], s1.at[n], r1.at[n],
+                device_id={"ctx": peer, "head": half}).start()
+
+    pairs = ((q_ref, qo_ref), (do_ref, doo_ref))
+    moves = []
+    for e, (src, dst) in enumerate(pairs):
+        place = dst.at[:, pl.ds(half * part, part)]
+        for i in range(1, halves):
+            other = lax.rem(half + i, halves)
+            move = pltpu.make_async_remote_copy(
+                src.at[pl.ds(other * heads, heads)], place, xs.at[e, i - 1], xr.at[e, i - 1],
+                device_id={"ctx": me, "head": other})
+            move.start()
+            moves.append(move)
+        pltpu.make_async_copy(src.at[pl.ds(half * heads, heads)], stage.at[e], xl.at[e]).start()
+
+    for n in range(heads):
+        held[n][me] = kv_ref[n, me]
+
+    for e, (src, dst) in enumerate(pairs):
+        pltpu.make_async_copy(src.at[pl.ds(half * heads, heads)], stage.at[e], xl.at[e]).wait()
+        pltpu.make_async_copy(stage.at[e], dst.at[:, pl.ds(half * part, part)], xl.at[e]).start()
+
+    for n in range(heads):
+        pltpu.make_async_remote_copy(
+            kv_ref.at[n, pl.ds(0, blocks - 1)], held[n].at[pl.ds(0, blocks - 1)], s1.at[n], r1.at[n],
+            device_id={"ctx": me, "head": half}).wait_recv()
+
+        @pl.loop(0, blocks)
+        def _(dest):
+            for j in range(2):
+                send[n, dest, j] = held[n][sel_ref[dest, j]]
+
+        @pl.loop(1, blocks)
+        def _(i):
+            dest = lax.rem(me + i, blocks)
+            pltpu.make_async_remote_copy(
+                send.at[n, dest], near_ref.at[n, :, me], s2.at[n], r2.at[n],
+                device_id={"ctx": dest, "head": half}).start()
+
+        pltpu.make_async_copy(send.at[n, me], near_ref.at[n, :, me], local2.at[n]).start()
+
+    for n in range(heads):
+        pltpu.make_async_copy(send.at[n, me], near_ref.at[n, :, me], local2.at[n]).wait()
+        done1 = pltpu.make_async_remote_copy(
+            kv_ref.at[n, pl.ds(0, blocks - 1)], held[n].at[pl.ds(0, blocks - 1)], s1.at[n], r1.at[n],
+            device_id={"ctx": me, "head": half})
+        done1.wait_send()
+        done2 = pltpu.make_async_remote_copy(
+            send.at[n, pl.ds(0, blocks - 1)], near_ref.at[n, :, pl.ds(0, blocks - 1)], s2.at[n], r2.at[n],
+            device_id={"ctx": me, "head": half})
+        done2.wait_send()
+        done2.wait_recv()
+    for move in moves:
+        move.wait()
+    for e, (src, dst) in enumerate(pairs):
+        pltpu.make_async_copy(stage.at[e], dst.at[:, pl.ds(half * part, part)], xl.at[e]).wait()
+
+
+def fetch(selected, kv, q, do, blocks, halves):
+    heads, _, piece, size = kv.shape
+    full, part, rows, _ = q.shape
+    whole = pl.BlockSpec(memory_space=pltpu.VMEM)
+    far = pl.BlockSpec(memory_space=pl.ANY)
+    mixed = jax.ShapeDtypeStruct((heads, part * halves, rows, size), BF16)
+    dma = pltpu.SemaphoreType.DMA
+    return pl.pallas_call(
+        functools.partial(fetch_kernel, blocks, halves),
+        in_specs=[pl.BlockSpec(memory_space=pltpu.SMEM), whole, far, far],
+        out_specs=[far, far, far],
+        out_shape=[jax.ShapeDtypeStruct((heads, 2, blocks, piece, size), BF16), mixed, mixed],
+        scratch_shapes=[
+            pltpu.VMEM((heads, blocks, 2, piece, size), BF16),
+            pltpu.VMEM((2, heads, part, rows, size), BF16),
+            dma((heads,)), dma((heads,)), dma((heads,)), dma((heads,)), dma((heads,)),
+            dma((2, halves - 1)), dma((2, halves - 1)), dma((2,)),
+        ] + [pltpu.VMEM((blocks, piece, size), BF16)] * heads,
+        compiler_params=pltpu.CompilerParams(collective_id=0, has_side_effects=True,
+                                             vmem_limit_bytes=32 * 2**20),
+    )(selected, kv, q, do)
+
+
+def return_kernel(blocks, halves, sel_ref, dnear_ref, out_ref, dq_ref, ret_ref, oo_ref, dqo_ref,
+                  arrived, home, stage, s1, r1, s2, r2, local1, local2, xs, xr, xl):
+    me, half = lax.axis_index("ctx"), lax.axis_index("head")
+    heads = dnear_ref.shape[0]
+    part = out_ref.shape[1] // halves
+    greet(blocks, halves)
+
+    def own_first(n):
+        return pltpu.make_async_copy(dnear_ref.at[n, :, me], arrived.at[n, me], local1.at[n])
+
+    def own_last(n):
+        return pltpu.make_async_copy(home.at[n, me], ret_ref.at[n, me], local2.at[n])
+
+    for n in range(heads):
+        @pl.loop(1, blocks)
+        def _(i):
+            peer = lax.rem(me + i, blocks)
+            pltpu.make_async_remote_copy(
+                dnear_ref.at[n, :, peer], arrived.at[n, me], s1.at[n], r1.at[n],
+                device_id={"ctx": peer, "head": half}).start()
+
+        own_first(n).start()
+
+    pairs = ((out_ref, oo_ref), (dq_ref, dqo_ref))
+    moves = []
+    for e, (src, dst) in enumerate(pairs):
+        place = dst.at[pl.ds(half * heads, heads)]
+        for i in range(1, halves):
+            other = lax.rem(half + i, halves)
+            move = pltpu.make_async_remote_copy(
+                src.at[:, pl.ds(other * part, part)], place, xs.at[e, i - 1], xr.at[e, i - 1],
+                device_id={"ctx": me, "head": other})
+            move.start()
+            moves.append(move)
+        pltpu.make_async_copy(src.at[:, pl.ds(half * part, part)], stage.at[e], xl.at[e]).start()
+    for e, (src, dst) in enumerate(pairs):
+        pltpu.make_async_copy(src.at[:, pl.ds(half * part, part)], stage.at[e], xl.at[e]).wait()
+        pltpu.make_async_copy(stage.at[e], dst.at[pl.ds(half * heads, heads)], xl.at[e]).start()
+
+    def first(n):
+        return pltpu.make_async_remote_copy(
+            dnear_ref.at[n, :, pl.ds(0, blocks - 1)], arrived.at[n, pl.ds(0, blocks - 1)], s1.at[n], r1.at[n],
+            device_id={"ctx": me, "head": half})
+
+    def last(n):
+        return pltpu.make_async_remote_copy(
+            home.at[n, pl.ds(0, blocks - 1)], ret_ref.at[n, pl.ds(0, blocks - 1)], s2.at[n], r2.at[n],
+            device_id={"ctx": me, "head": half})
+
+    for n in range(heads):
+        first(n).wait_recv()
+        own_first(n).wait()
+
+        @pl.loop(0, blocks)
+        def _(s):
+            def add(b, total):
+                for j in range(2):
+                    mine = (sel_ref[b, j] == s).astype(F32)
+                    total = total + arrived[n, b, j].astype(F32) * mine
+                return total
+
+            total = lax.fori_loop(s, blocks, add, jnp.zeros(home.shape[2:], F32))
+            home[n, s] = total.astype(BF16)
+
+        @pl.loop(1, blocks)
+        def _(i):
+            dest = lax.rem(me + i, blocks)
+            pltpu.make_async_remote_copy(
+                home.at[n, dest], ret_ref.at[n, me], s2.at[n], r2.at[n],
+                device_id={"ctx": dest, "head": half}).start()
+
+        own_last(n).start()
+
+    for n in range(heads):
+        own_last(n).wait()
+        first(n).wait_send()
+        last(n).wait_send()
+        last(n).wait_recv()
+    for move in moves:
+        move.wait()
+    for e, (src, dst) in enumerate(pairs):
+        pltpu.make_async_copy(stage.at[e], dst.at[pl.ds(half * heads, heads)], xl.at[e]).wait()
+
+
+def give_back(selected, dnear, out, dq, blocks, halves):
+    heads, _, _, piece, size = dnear.shape
+    _, group, rows, _ = out.shape
+    far = pl.BlockSpec(memory_space=pl.ANY)
+    mixed = jax.ShapeDtypeStruct((heads * halves, group // halves, rows, size), BF16)
+    dma = pltpu.SemaphoreType.DMA
+    return pl.pallas_call(
+        functools.partial(return_kernel, blocks, halves),
+        in_specs=[pl.BlockSpec(memory_space=pltpu.SMEM), far, far, far],
+        out_specs=[far, far, far],
+        out_shape=[jax.ShapeDtypeStruct((heads, blocks, piece, size), BF16), mixed, mixed],
+        scratch_shapes=[
+            pltpu.VMEM((heads, blocks, 2, piece, size), BF16),
+            pltpu.VMEM((heads, blocks, piece, size), BF16),
+            pltpu.VMEM((2, heads, group // halves, rows, size), BF16),
+            dma((heads,)), dma((heads,)), dma((heads,)), dma((heads,)), dma((heads,)), dma((heads,)),
+            dma((2, halves - 1)), dma((2, halves - 1)), dma((2,)),
+        ],
+        compiler_params=pltpu.CompilerParams(collective_id=1, has_side_effects=True,
+                                             vmem_limit_bytes=32 * 2**20),
+    )(selected, dnear, out, dq)
+
+
 def on_device(queries, keys, values, output_gradient, selected):
     rows, kv_count, size = keys.shape
-    blocks = lax.axis_size("ctx")
-    own_heads = kv_count // lax.axis_size("head")
+    blocks, halves = lax.axis_size("ctx"), lax.axis_size("head")
+    own_heads = kv_count // halves
     me = lax.axis_index("ctx")
     half = lax.axis_index("head")
-
-    def to_heads(x):
-        x = lax.all_to_all(x, "head", split_axis=2, concat_axis=1, tiled=True)
-        return jnp.transpose(x, (2, 1, 0, 3))
-
-    def from_heads(x):
-        x = jnp.transpose(x, (2, 1, 0, 3))
-        return lax.all_to_all(x, "head", split_axis=1, concat_axis=2, tiled=True)
-
-    q, do = to_heads(queries), to_heads(output_gradient)
+    piece = 2 * rows // blocks
     own = jnp.stack([keys, values])
     own = lax.dynamic_slice_in_dim(own, half * own_heads, own_heads, 2)
-    own = jnp.transpose(own, (0, 2, 1, 3))
-    piece = 2 * own_heads * rows // blocks
-    flat = own.reshape(blocks, piece, size)
-    held = lax.all_to_all(flat, "ctx", split_axis=0, concat_axis=0, tiled=True)
-    near = lax.all_to_all(held[jnp.transpose(selected)], "ctx", split_axis=1, concat_axis=1, tiled=True)
-    near = near.reshape((2,) + own.shape)
+    own = jnp.transpose(own, (2, 0, 1, 3))
+    q, do = jnp.transpose(queries, (2, 1, 0, 3)), jnp.transpose(output_gradient, (2, 1, 0, 3))
+    near, q, do = fetch(selected, own.reshape(own_heads, blocks, piece, size), q, do, blocks, halves)
+    near = near.reshape(own_heads, 2, 2, rows, size)
     visible = (lax.dynamic_index_in_dim(selected, me, 0, keepdims=False) < me).astype(jnp.int32)
     out, dq, dnear, down = attend(visible, q, do, near, own)
-    back = lax.all_to_all(dnear.reshape(2, blocks, piece, size), "ctx", split_axis=1, concat_axis=1, tiled=True)
-    owners = (jnp.transpose(selected)[:, :, None] == jnp.arange(blocks, dtype=jnp.int32)).astype(BF16)
-    home = jnp.einsum("jrb,jrpd->bpd", owners, back, preferred_element_type=F32).astype(BF16)
-    home = lax.all_to_all(home, "ctx", split_axis=0, concat_axis=0, tiled=True)
-    grads = (home.reshape(own.shape).astype(F32) + down).astype(BF16)
-    grads = jnp.transpose(grads, (0, 2, 1, 3))
-    return from_heads(out), from_heads(dq), grads[0], grads[1]
+    ret, out, dq = give_back(
+        selected, dnear.reshape(own_heads, 2, blocks, piece, size), out, dq, blocks, halves)
+    grads = (ret.reshape(own.shape).astype(F32) + down).astype(BF16)
+    grads = jnp.transpose(grads, (1, 2, 0, 3))
+    return jnp.transpose(out, (2, 1, 0, 3)), jnp.transpose(dq, (2, 1, 0, 3)), grads[0], grads[1]
 
 
 def solution(mesh):

time: 171 us -> 139 us (0.81)
  Pallas kernels: 34.9 us -> 120 us
  waiting for transfers between devices: 65.4 us -> 0 us
  starting transfers between devices: 31.7 us -> 0 us
  blocking collectives: 9.94 us -> 0 us
  local copies, waits for them, and re-layouts: 24.4 us -> 15.8 us
    pallas_call x0 -> x2, Pallas kernels: none -> 85.6 us  [the longest x1 47.3 us: give_back(): pl.pallas_call(functools.partial(return_kernel, blocks, halves), in_specs...]
    all_to_all x6 -> x0, waiting for transfers between devices: 65.4 us -> none  [the longest x1 21 us: on_device(): lax.all_to_all(dnear.reshape(2, blocks, piece, size), 'ctx', split_axis=1...]
    all_to_all x6 -> x0, starting transfers between devices: 31.7 us -> none  [the longest x1 8.47 us: on_device(): held = lax.all_to_all(flat, 'ctx', split_axis=0, concat_axis=0, tiled=True)]
    all_to_all x2 -> x0, blocking collectives: 9.94 us -> none  [the longest x1 5.38 us: to_heads(): x = lax.all_to_all(x, 'head', split_axis=2, concat_axis=1, tiled=True)]
    unnamed x20 -> x25, local copies, waits for them, and re-layouts: 6.33 us -> 14.1 us
    all_to_all x5 -> x0, local copies, waits for them, and re-layouts: 7.23 us -> none  [the longest x2 4.1 us: from_heads(): return lax.all_to_all(x, 'head', split_axis=1, concat_axis=2, tiled=True)]
    gather x2 -> x0, local copies, waits for them, and re-layouts: 4.08 us -> none  [on_device(): held[jnp.transpose(selected)]]
    reshape x1 -> x0, local copies, waits for them, and re-layouts: 3.28 us -> none  [on_device(): dnear.reshape(2, blocks, piece, size)]
  transfers between devices with their start and end apart: 6 -> 0, of which waited for: 5 -> 0; matrix products, arithmetic and copies ran while one was open for 10% -> 0% of each run, Pallas kernels for 0% -> 0%
where the time goes in v2:
time: 139 us
  Pallas kernels  120 us (86%)
  local copies, waits for them, and re-layouts  15.8 us (11%)
  other arithmetic  1.75 us (1%)
    pallas_call x1, Pallas kernels, give_back(): pl.pallas_call(functools.partial(return_kernel, blocks, halves), in_specs...  47.3 us
    pallas_call x1, Pallas kernels, fetch(): pl.pallas_call(functools.partial(fetch_kernel, blocks, halves), in_specs=...  38.3 us
    pallas_call x1, Pallas kernels, attend(): pl.pallas_call(functools.partial(attend_kernel, tile), grid_spec=pltpu.Pr...  34.8 us
    unnamed x25, local copies, waits for them, and re-layouts  14.1 us

profile of v2, /device:TPU:0, one launch (start us, length us, event | category | flops | bytes accessed | tf_op | source)
XLA Modules:
  0.0 138.7 jit_solution(3027951285666274646)
XLA Ops:
  0.6 0.0 copy-start.9
  0.6 0.7 copy-done.9
  1.3 0.7 fusion.3.vis_ref
  2.0 0.1 copy.14.sel_ref
  2.1 1.3 copy_bitcast_fusion.2
  3.4 0.0 copy-start.8
  3.4 0.9 fusion.4.own_ref
  4.3 0.0 copy-start.7
  4.3 0.1 fusion.2
  4.4 0.5 copy-done.8
  4.9 0.8 copy-done.7
  5.6 0.4 copy_bitcast_fusion
  6.0 38.3 %shard_map.84 = (bf16[2,2,16,64,128]{4,3,2,1,0:T(8,128)(2,1)S(1)}, bf16[2,4,512,128]{3,2,1,0:T(8,128)(2,1)S(1)}, bf16[2,4,512,128]{3,2,1,0:T(8,128)(2,1)S(1)}) custom-call(s32[16,2]{1,0:T(8,128)S(1)} %copy.14.sel_ref, bf16[2,16,64,128]{3,2,1,0:T(8,128)(2,1)S(1)} %bitcast.26, bf16[4,2,512,128]{3,2,1,0:T(8,128)(2,1)S(1)} %get-tuple-element.33.q_ref, ...), custom_call_target="tpu_custom_call" | custom-call | tf_op jit(solution)/shard_map/pallas_call | solution.py:223
  44.3 0.0 copy-start.3
  44.3 1.0 copy-done.3
  45.3 0.0 copy-start.4
  45.3 1.0 copy-done.4
  46.3 0.0 copy-start.5
  46.3 1.0 copy-done.5
  47.2 34.8 %shard_map.85 = (bf16[2,4,512,128]{3,2,1,0:T(8,128)(2,1)}, bf16[2,4,512,128]{3,2,1,0:T(8,128)(2,1)}, bf16[2,2,2,512,128]{4,3,2,1,0:T(8,128)(2,1)}, f32[2,2,512,128]{3,2,1,0:T(8,128)}) custom-call(s32[2]{0:T(128)} %fusion.3.vis_ref, bf16[2,4,512,128]{3,2,1,0:T(8,128)(2,1)} %copy-done.4, bf16[2,4,512,128]{3,2,1,0:T(8,128)(2,1)} %copy-done.5, ...), custom_call_target="tpu_custom_call" | custom-call | tf_op jit(solution)/shard_map/pallas_call | solution.py:108
  82.0 0.0 copy-start
  82.0 1.2 copy-done
  83.3 0.0 copy-start.1
  83.3 1.2 copy-done.1
  84.5 0.0 copy-start.2
  84.5 1.2 copy-done.2
  85.7 0.0 copy-start.6
  85.7 47.3 %shard_map.86 = (bf16[2,16,64,128]{3,2,1,0:T(8,128)(2,1)S(1)}, bf16[4,2,512,128]{3,2,1,0:T(8,128)(2,1)S(1)}, bf16[4,2,512,128]{3,2,1,0:T(8,128)(2,1)S(1)}) custom-call(s32[16,2]{1,0:T(8,128)S(1)} %copy.14.sel_ref, bf16[2,2,16,64,128]{4,3,2,1,0:T(8,128)(2,1)S(1)} %bitcast.27, bf16[2,4,512,128]{3,2,1,0:T(8,128)(2,1)S(1)} %copy-done, ...), custom_call_target="tpu_custom_call" | custom-call | tf_op jit(solution)/shard_map/pallas_call | solution.py:329
  133.0 0.0 copy-done.6
  133.0 0.1 fusion.1
  133.2 1.8 %copy.15 = bf16[512,2,4,128]{3,2,1,0:T(4,128)(2,1)} copy(bf16[512,2,4,128]{3,0,1,2:T(8,128)(2,1)S(1)} %bitcast.29) | data formatting | bytes 2097152
  134.9 1.8 %copy.16 = bf16[512,2,4,128]{3,2,1,0:T(4,128)(2,1)} copy(bf16[512,2,4,128]{3,0,1,2:T(8,128)(2,1)S(1)} %bitcast.28) | data formatting | bytes 2097152
  136.8 1.0 copy.18
  137.7 1.0 copy.17
  (1 shorter events, 0.0 us)
Async XLA Ops:
  0.6 0.7 copy-start.9
  3.4 1.4 %copy-start.8 = (bf16[512,2,4,128]{3,2,1,0:T(4,128)(2,1)S(1)}, bf16[512,2,4,128]{3,2,1,0:T(4,128)(2,1)}, u32[]{:S(2)}) copy-start(bf16[512,2,4,128]{3,2,1,0:T(4,128)(2,1)} %param.5) | copy-start | bytes 3145732
  4.3 1.3 copy-start.7
  44.3 1.0 copy-start.3
  45.3 1.0 copy-start.4
  46.3 1.0 copy-start.5
  82.0 1.2 copy-start
  83.3 1.2 copy-start.1
  84.5 1.2 copy-start.2
  85.7 47.3 %copy-start.6 = (f32[2,2,512,128]{3,2,1,0:T(8,128)S(1)}, f32[2,2,512,128]{3,2,1,0:T(8,128)}, u32[]{:S(2)}) copy-start(f32[2,2,512,128]{3,2,1,0:T(8,128)} %get-tuple-element.23) | copy-start | bytes 3145732

commit v3 on v1

v3 whole, which is shorter than its diff:
```python
import functools
import math

import jax
import jax.numpy as jnp
from jax import lax
from jax.experimental import pallas as pl
from jax.experimental.pallas import tpu as pltpu
from jax.sharding import PartitionSpec as P

F32 = jnp.float32
BF16 = jnp.bfloat16


def dot_nt(a, b):
    return lax.dot_general(a, b, (((1,), (1,)), ((), ())), preferred_element_type=F32)


def dot_nn(a, b):
    return lax.dot_general(a, b, (((1,), (0,)), ((), ())), preferred_element_type=F32)


def greet(blocks, halves):
    me, half = lax.axis_index("ctx"), lax.axis_index("head")
    barrier = pltpu.get_barrier_semaphore()

    @pl.loop(1, blocks)
    def _(i):
        pl.semaphore_signal(barrier, inc=1, device_id={"ctx": lax.rem(me + i, blocks), "head": half})

    for i in range(1, halves):
        pl.semaphore_signal(barrier, inc=1, device_id={"ctx": me, "head": lax.rem(half + i, halves)})
    pl.semaphore_wait(barrier, blocks - 1 + halves - 1)


def attend_tile(t, tile, scale, visible, q, do, keys, values, kt_ref, vt_ref, dk_ref, dv_ref):
    rows, size = keys.shape[1], keys.shape[2]
    factor = scale * math.log2(math.e)
    do_t = do.astype(F32).T
    do_tb = do_t.astype(BF16)
    q_tb = q.astype(F32).T.astype(BF16)
    counts = (rows, rows, (t + 1) * tile)
    scores, tops = [], []
    for j in range(3):
        s = dot_nn(keys[j, 0:counts[j], :], q_tb) * factor
        if j == 2:
            key_at = lax.broadcasted_iota(jnp.int32, s.shape, 0)
            query_at = lax.broadcasted_iota(jnp.int32, s.shape, 1) + t * tile
            s = jnp.where(key_at <= query_at, s, -jnp.inf)
        top = jnp.max(s, axis=0, keepdims=True)
        if j < 2:
            top = jnp.where(visible[j], top, -jnp.inf)
        scores.append(s)
        tops.append(top)
    top = jnp.maximum(jnp.maximum(tops[0], tops[1]), tops[2])
    total = jnp.zeros_like(top)
    weights = []
    for j in range(3):
        shift = jnp.where(visible[j], top, jnp.inf) if j < 2 else top
        e = jnp.exp2(scores[j] - shift)
        total = total + jnp.sum(e, axis=0, keepdims=True)
        weights.append(e)
    inverse = 1.0 / total
    out_t = jnp.zeros((size, tile), F32)
    lows, probs = [], []
    for j in range(3):
        p = weights[j] * inverse
        low = p.astype(BF16)
        probs.append(p)
        lows.append(low)
        out_t = out_t + dot_nn(vt_ref[:, j * rows:j * rows + counts[j]], low)
    out_low = out_t.astype(BF16).astype(F32)
    row_dot = jnp.sum(do_t * out_low, axis=0, keepdims=True)
    dq_t = jnp.zeros((size, tile), F32)
    for j in range(3):
        dp = dot_nn(values[j, 0:counts[j], :], do_tb)
        ds = (probs[j] * (dp - row_dot)).astype(BF16)
        dq_t = dq_t + dot_nn(kt_ref[:, j * rows:j * rows + counts[j]], ds)
        dk_ref[j, 0:counts[j], :] += dot_nn(ds, q)
        dv_ref[j, 0:counts[j], :] += dot_nn(lows[j], do)
    return out_low.T.astype(BF16), (dq_t * scale).T.astype(BF16)


def step_kernel(blocks, halves, tile, sel_ref, kv_ref, own_ref, q_ref, do_ref, grads_ref, oo_ref, dqo_ref,
                qv, dov, near, send, ks, vs, kt, vt, dk, dv, down, outv, dqv, dnear, arrived, home, ret,
                s1, r1, s2, r2, xs, xr, xl, b1, c1, b2, c2, ys, yr, yl, *held):
    me, half = lax.axis_index("ctx"), lax.axis_index("head")
    heads, group, rows, size = qv.shape
    part = group // halves
    piece = kv_ref.shape[2]
    scale = size ** -0.5
    visible = [sel_ref[me, j] < me for j in range(2)]
    here = {"ctx": me, "head": half}
    greet(blocks, halves)

    def send_all(make):
        @pl.loop(1, blocks)
        def _(i):
            make(lax.rem(me + i, blocks)).start()

    for n in range(heads):
        send_all(lambda peer: pltpu.make_async_remote_copy(
            kv_ref.at[n, peer], held[n].at[me], s1.at[n], r1.at[n], device_id={"ctx": peer, "head": half}))

    moves = []
    for e, (src, dst) in enumerate(((q_ref, qv), (do_ref, dov))):
        place = dst.at[:, pl.ds(half * part, part)]
        for i in range(1, halves):
            other = lax.rem(half + i, halves)
            moves.append(pltpu.make_async_remote_copy(
                src.at[pl.ds(other * heads, heads)], place, xs.at[e, i - 1], xr.at[e, i - 1],
                device_id={"ctx": me, "head": other}))
        moves.append(pltpu.make_async_copy(src.at[pl.ds(half * heads, heads)], place, xl.at[e]))
    for move in moves:
        move.start()

    def fetch_first(n):
        return pltpu.make_async_remote_copy(
            kv_ref.at[n, pl.ds(0, blocks - 1)], held[n].at[pl.ds(0, blocks - 1)], s1.at[n], r1.at[n],
            device_id=here)

    def fetch_last(n):
        return pltpu.make_async_remote_copy(
            send.at[n, pl.ds(0, blocks - 1)], near.at[n, :, pl.ds(0, blocks - 1)], s2.at[n], r2.at[n],
            device_id=here)

    for n in range(heads):
        held[n][me] = kv_ref[n, me]
        fetch_first(n).wait_recv()

        @pl.loop(0, blocks)
        def _(dest):
            for j in range(2):
                send[n, dest, j] = held[n][sel_ref[dest, j]]

        send_all(lambda dest: pltpu.make_async_remote_copy(
            send.at[n, dest], near.at[n, :, me], s2.at[n], r2.at[n], device_id={"ctx": dest, "head": half}))
        for j in range(2):
            near[n, j, me] = held[n][sel_ref[me, j]]

    for move in moves:
        move.wait()

    def back_first(n):
        return pltpu.make_async_remote_copy(
            dnear.at[n, :, pl.ds(0, blocks - 1)], arrived.at[n, pl.ds(0, blocks - 1)], b1.at[n], c1.at[n],
            device_id=here)

    def back_last(n):
        return pltpu.make_async_remote_copy(
            home.at[n, pl.ds(0, blocks - 1)], ret.at[n, pl.ds(0, blocks - 1)], b2.at[n], c2.at[n],
            device_id=here)

    def collect(n):
        back_first(n).wait_recv()

        @pl.loop(0, blocks)
        def _(s):
            def add(b, total):
                for j in range(2):
                    mine = (sel_ref[b, j] == s).astype(F32)
                    total = total + arrived[n, b, j].astype(F32) * mine
                return total

            total = lax.fori_loop(s, blocks, add, jnp.zeros((piece, size), F32))
            home[n, s] = total.astype(BF16)

        send_all(lambda dest: pltpu.make_async_remote_copy(
            home.at[n, dest], ret.at[n, me], b2.at[n], c2.at[n], device_id={"ctx": dest, "head": half}))
        ret[n, me] = home[n, me]

    def results(n):
        made = []
        for e, (src, dst) in enumerate(((outv, oo_ref), (dqv, dqo_ref))):
            place = dst.at[half * heads + n]
            for i in range(1, halves):
                other = lax.rem(half + i, halves)
                made.append(pltpu.make_async_remote_copy(
                    src.at[n, pl.ds(other * part, part)], place, ys.at[n, e, i - 1], yr.at[n, e, i - 1],
                    device_id={"ctx": me, "head": other}))
            made.append(pltpu.make_async_copy(src.at[n, pl.ds(half * part, part)], place, yl.at[n, e]))
        return made

    def join(x):
        if piece % 16 == 0:
            return x.reshape(rows, size)
        return x.astype(F32).reshape(rows, size).astype(BF16)

    pieces = blocks // 2

    @pl.loop(0, heads * group)
    def _(at):
        n = at // group
        g = at % group

        @pl.when(g == 0)
        def _():
            fetch_last(n).wait_recv()
            for j in range(3):
                if j < 2:
                    k, v = join(near[n, j, 0:pieces]), join(near[n, j, pieces:2 * pieces])
                else:
                    k, v = own_ref[n, 0], own_ref[n, 1]
                ks[j] = k
                vs[j] = v
                kt[:, j * rows:(j + 1) * rows] = k.astype(F32).T.astype(BF16)
                vt[:, j * rows:(j + 1) * rows] = v.astype(F32).T.astype(BF16)
            dk[...] = jnp.zeros_like(dk)
            dv[...] = jnp.zeros_like(dv)

        for t in range(rows // tile):
            span = slice(t * tile, (t + 1) * tile)
            out, dq = attend_tile(t, tile, scale, visible, qv[n, g, span, :], dov[n, g, span, :],
                                  ks, vs, kt, vt, dk, dv)
            outv[n, g, span, :] = out
            dqv[n, g, span, :] = dq

        @pl.when(g == group - 1)
        def _():
            for j in range(2):
                dnear[n, j, 0:pieces] = (dk[j] * scale).reshape(pieces, piece, size).astype(BF16)
                dnear[n, j, pieces:2 * pieces] = dv[j].reshape(pieces, piece, size).astype(BF16)
            down[n, 0:pieces] = (dk[2] * scale).reshape(pieces, piece, size)
            down[n, pieces:2 * pieces] = dv[2].reshape(pieces, piece, size)
            send_all(lambda peer: pltpu.make_async_remote_copy(
                dnear.at[n, :, peer], arrived.at[n, me], b1.at[n], c1.at[n],
                device_id={"ctx": peer, "head": half}))
            for j in range(2):
                arrived[n, me, j] = dnear[n, j, me]
            for move in results(n):
                move.start()

        @pl.when((n > 0) & (g == group - 2))
        def _():
            collect(n - 1)

    collect(heads - 1)
    for n in range(heads):
        fetch_first(n).wait_send()
        fetch_last(n).wait_send()
        back_first(n).wait_send()
        for move in results(n):
            move.wait()
    for n in range(heads):
        back_last(n).wait_send()
        back_last(n).wait_recv()
        grads_ref[n] = (ret[n].astype(F32) + down[n]).astype(BF16)


def step(selected, kv, own, q, do, blocks, halves):
    heads, _, piece, size = kv.shape
    full, part, rows, _ = q.shape
    group = part * halves
    tile = min(256, rows)
    near = pl.BlockSpec(memory_space=pltpu.VMEM)
    far = pl.BlockSpec(memory_space=pl.ANY)
    dma = pltpu.SemaphoreType.DMA
    vmem = pltpu.VMEM
    return pl.pallas_call(
        functools.partial(step_kernel, blocks, halves, tile),
        in_specs=[pl.BlockSpec(memory_space=pltpu.SMEM), near, near, far, far],
        out_specs=[near, far, far],
        out_shape=[jax.ShapeDtypeStruct(kv.shape, BF16), jax.ShapeDtypeStruct(q.shape, BF16),
                   jax.ShapeDtypeStruct(q.shape, BF16)],
        scratch_shapes=[
            vmem((heads, group, rows, size), BF16),
            vmem((heads, group, rows, size), BF16),
            vmem((heads, 2, blocks, piece, size), BF16),
            vmem((heads, blocks, 2, piece, size), BF16),
            vmem((3, rows, size), BF16),
            vmem((3, rows, size), BF16),
            vmem((size, 3 * rows), BF16),
            vmem((size, 3 * rows), BF16),
            vmem((3, rows, size), F32),
            vmem((3, rows, size), F32),
            vmem((heads, blocks, piece, size), F32),
            vmem((heads, group, rows, size), BF16),
            vmem((heads, group, rows, size), BF16),
            vmem((heads, 2, blocks, piece, size), BF16),
            vmem((heads, blocks, 2, piece, size), BF16),
            vmem((heads, blocks, piece, size), BF16),
            vmem((heads, blocks, piece, size), BF16),
            dma((heads,)), dma((heads,)), dma((heads,)), dma((heads,)),
            dma((2, halves - 1)), dma((2, halves - 1)), dma((2,)),
            dma((heads,)), dma((heads,)), dma((heads,)), dma((heads,)),
            dma((heads, 2, halves - 1)), dma((heads, 2, halves - 1)), dma((heads, 2)),
        ] + [vmem((blocks, piece, size), BF16)] * heads,
        compiler_params=pltpu.CompilerParams(collective_id=0, has_side_effects=True,
                                             vmem_limit_bytes=56 * 2**20),
    )(selected, kv, own, q, do)


def on_device(queries, keys, values, output_gradient, selected):
    rows, kv_count, size = keys.shape
    blocks, halves = lax.axis_size("ctx"), lax.axis_size("head")
    own_heads = kv_count // halves
    half = lax.axis_index("head")
    piece = 2 * rows // blocks
    own = jnp.stack([keys, values])
    own = lax.dynamic_slice_in_dim(own, half * own_heads, own_heads, 2)
    own = jnp.transpose(own, (2, 0, 1, 3))
    q, do = jnp.transpose(queries, (2, 1, 0, 3)), jnp.transpose(output_gradient, (2, 1, 0, 3))
    grads, out, dq = step(selected, own.reshape(own_heads, blocks, piece, size), own, q, do, blocks, halves)
    grads = jnp.transpose(grads.reshape(own.shape), (1, 2, 0, 3))
    return jnp.transpose(out, (2, 1, 0, 3)), jnp.transpose(dq, (2, 1, 0, 3)), grads[0], grads[1]


def solution(mesh):
    return jax.shard_map(
        on_device,
        mesh=mesh,
        in_specs=(
            P("ctx", "head", None, None),
            P("ctx", None, None),
            P("ctx", None, None),
            P("ctx", "head", None, None),
            P(),
        ),
        out_specs=(
            P("ctx", "head", None, None),
            P("ctx", "head", None, None),
            P("ctx", "head", None),
            P("ctx", "head", None),
        ),
        check_vma=False,
    )
```

time: 171 us -> 108 us (0.63)
  waiting for transfers between devices: 65.4 us -> 0 us
  Pallas kernels: 34.9 us -> 94.1 us
  starting transfers between devices: 31.7 us -> 0 us
  local copies, waits for them, and re-layouts: 24.4 us -> 11.6 us
  blocking collectives: 9.94 us -> 0 us
    all_to_all x6 -> x0, waiting for transfers between devices: 65.4 us -> none  [the longest x1 21 us: on_device(): lax.all_to_all(dnear.reshape(2, blocks, piece, size), 'ctx', split_axis=1...]
    pallas_call x1, Pallas kernels: 34.9 us -> 94.1 us  [step(): pl.pallas_call(functools.partial(step_kernel, blocks, halves, tile), in_s...]
    all_to_all x6 -> x0, starting transfers between devices: 31.7 us -> none  [the longest x1 8.47 us: on_device(): held = lax.all_to_all(flat, 'ctx', split_axis=0, concat_axis=0, tiled=True)]
    all_to_all x2 -> x0, blocking collectives: 9.94 us -> none  [the longest x1 5.38 us: to_heads(): x = lax.all_to_all(x, 'head', split_axis=2, concat_axis=1, tiled=True)]
    all_to_all x5 -> x0, local copies, waits for them, and re-layouts: 7.23 us -> none  [the longest x2 4.1 us: from_heads(): return lax.all_to_all(x, 'head', split_axis=1, concat_axis=2, tiled=True)]
    gather x2 -> x0, local copies, waits for them, and re-layouts: 4.08 us -> none  [on_device(): held[jnp.transpose(selected)]]
    reshape x1, local copies, waits for them, and re-layouts: 3.28 us -> 0.54 us  [on_device(): grads = jnp.transpose(grads.reshape(own.shape), (1, 2, 0, 3))]
    unnamed x20 -> x13, local copies, waits for them, and re-layouts: 6.33 us -> 6.87 us
  transfers between devices with their start and end apart: 6 -> 0, of which waited for: 5 -> 0; matrix products, arithmetic and copies ran while one was open for 10% -> 0% of each run, Pallas kernels for 0% -> 0%
where the time goes in v3:
time: 108 us
  Pallas kernels  94.1 us (87%)
  local copies, waits for them, and re-layouts  11.6 us (11%)
  other arithmetic  1.72 us (2%)
    pallas_call x1, Pallas kernels, step(): pl.pallas_call(functools.partial(step_kernel, blocks, halves, tile), in_s...  94.1 us
    unnamed x13, local copies, waits for them, and re-layouts  6.87 us

profile of v3, /device:TPU:0, one launch (start us, length us, event | category | flops | bytes accessed | tf_op | source)
XLA Modules:
  0.0 108.1 jit_solution(7403538836978403359)
XLA Ops:
  0.6 0.0 copy-start.4
  0.6 0.7 copy-done.4
  1.3 0.7 copy.13.sel_ref
  2.0 1.3 %copy_bitcast_fusion.3 = (bf16[1,512,4,128]{3,1,0,2:T(8,128)(2,1)S(1)}, bf16[1,512,4,128]{3,1,0,2:T(8,128)(2,1)S(1)}) fusion(bf16[512,4,128]{2,1,0:T(4,128)(2,1)} %param.7, bf16[512,4,128]{2,1,0:T(4,128)(2,1)} %param.6), kind=kLoop, calls=%fused_computation.6 | loop fusion | bytes 2097152 | tf_op jit(solution)/shard_map/stack | solution.py:299
  3.3 0.0 copy-start.2
  3.3 0.9 fusion.1.own_ref
  4.2 0.0 copy-start.1
  4.2 0.9 fusion
  5.1 0.0 copy-done.2
  5.1 0.6 copy-done.1
  5.7 1.7 %copy_bitcast_fusion = (bf16[4,2,512,128]{3,2,1,0:T(8,128)(2,1)}, bf16[4,2,512,128]{3,2,1,0:T(8,128)(2,1)}) fusion(bf16[512,2,4,128]{3,2,1,0:T(4,128)(2,1)S(1)} %copy-done.1, bf16[512,2,4,128]{3,2,1,0:T(4,128)(2,1)S(1)} %copy-done.2), kind=kLoop, calls=%fused_computation.2 | loop fusion | bytes 4194304 | tf_op jit(solution)/shard_map/transpose | solution.py:302
  7.4 94.1 %shard_map.84 = (bf16[2,16,64,128]{3,2,1,0:T(8,128)(2,1)}, bf16[4,2,512,128]{3,2,1,0:T(8,128)(2,1)}, bf16[4,2,512,128]{3,2,1,0:T(8,128)(2,1)}) custom-call(s32[16,2]{1,0:T(8,128)} %copy.13.sel_ref, bf16[2,16,64,128]{3,2,1,0:T(8,128)(2,1)} %bitcast.23, bf16[2,2,512,128]{3,2,1,0:T(8,128)(2,1)} %fusion.1.own_ref, ...), custom_call_target="tpu_custom_call" | custom-call | tf_op jit(solution)/shard_map/pallas_call | solution.py:259
  101.5 0.0 copy-start
  101.5 3.1 %copy.15 = bf16[512,2,4,128]{3,2,1,0:T(4,128)(2,1)} copy(bf16[512,2,4,128]{3,0,1,2:T(8,128)(2,1)} %bitcast.25) | data formatting | bytes 2097152
  104.6 0.0 copy-done
  104.6 0.0 copy-start.3
  104.6 1.8 %copy.16 = bf16[512,2,4,128]{3,2,1,0:T(4,128)(2,1)} copy(bf16[512,2,4,128]{3,0,1,2:T(8,128)(2,1)S(1)} %bitcast.24) | data formatting | bytes 2097152
  106.4 0.0 copy-done.3
  106.4 0.5 copy.22
  106.9 1.2 %slice_bitcast_fusion = (bf16[512,2,128]{2,1,0:T(2,128)(2,1)}, bf16[512,2,128]{2,1,0:T(2,128)(2,1)}) fusion(bf16[2,512,2,128]{3,2,1,0:T(2,128)(2,1)S(1)} %bitcast.22), kind=kLoop, calls=%fused_computation.8 | loop fusion | bytes 1048576 | tf_op jit(solution)/shard_map/squeeze | solution.py:305
Async XLA Ops:
  0.6 0.7 copy-start.4
  3.3 1.7 %copy-start.2 = (bf16[512,2,4,128]{3,2,1,0:T(4,128)(2,1)S(1)}, bf16[512,2,4,128]{3,2,1,0:T(4,128)(2,1)}, u32[]{:S(2)}) copy-start(bf16[512,2,4,128]{3,2,1,0:T(4,128)(2,1)} %param.5) | copy-start | bytes 3145732
  4.2 1.5 %copy-start.1 = (bf16[512,2,4,128]{3,2,1,0:T(4,128)(2,1)S(1)}, bf16[512,2,4,128]{3,2,1,0:T(4,128)(2,1)}, u32[]{:S(2)}) copy-start(bf16[512,2,4,128]{3,2,1,0:T(4,128)(2,1)} %param.8) | copy-start | bytes 3145732
  101.5 3.1 %copy-start = (bf16[4,2,512,128]{3,2,1,0:T(8,128)(2,1)S(1)}, bf16[4,2,512,128]{3,2,1,0:T(8,128)(2,1)}, u32[]{:S(2)}) copy-start(bf16[4,2,512,128]{3,2,1,0:T(8,128)(2,1)} %get-tuple-element.8) | copy-start | bytes 3145732
  104.6 1.8 %copy-start.3 = (bf16[2,16,64,128]{3,2,1,0:T(8,128)(2,1)S(1)}, bf16[2,16,64,128]{3,2,1,0:T(8,128)(2,1)}, u32[]{:S(2)}) copy-start(bf16[2,16,64,128]{3,2,1,0:T(8,128)(2,1)} %get-tuple-element.9) | copy-start | bytes 1572868

commit v4 on v3

--- a/solution.py
+++ b/solution.py
@@ -98,9 +98,11 @@
         def _(i):
             make(lax.rem(me + i, blocks)).start()
 
-    for n in range(heads):
+    def spread(n):
         send_all(lambda peer: pltpu.make_async_remote_copy(
             kv_ref.at[n, peer], held[n].at[me], s1.at[n], r1.at[n], device_id={"ctx": peer, "head": half}))
+
+    spread(0)
 
     moves = []
     for e, (src, dst) in enumerate(((q_ref, qv), (do_ref, dov))):
@@ -124,7 +126,7 @@
             send.at[n, pl.ds(0, blocks - 1)], near.at[n, :, pl.ds(0, blocks - 1)], s2.at[n], r2.at[n],
             device_id=here)
 
-    for n in range(heads):
+    def relay(n):
         held[n][me] = kv_ref[n, me]
         fetch_first(n).wait_recv()
 
@@ -135,8 +137,12 @@
 
         send_all(lambda dest: pltpu.make_async_remote_copy(
             send.at[n, dest], near.at[n, :, me], s2.at[n], r2.at[n], device_id={"ctx": dest, "head": half}))
+        if n + 1 < heads:
+            spread(n + 1)
         for j in range(2):
             near[n, j, me] = held[n][sel_ref[me, j]]
+
+    relay(0)
 
     for move in moves:
         move.wait()
@@ -151,18 +157,22 @@
             home.at[n, pl.ds(0, blocks - 1)], ret.at[n, pl.ds(0, blocks - 1)], b2.at[n], c2.at[n],
             device_id=here)
 
+    together = math.gcd(4, blocks)
+
     def collect(n):
         back_first(n).wait_recv()
 
         @pl.loop(0, blocks)
         def _(s):
-            def add(b, total):
-                for j in range(2):
-                    mine = (sel_ref[b, j] == s).astype(F32)
-                    total = total + arrived[n, b, j].astype(F32) * mine
+            def add(c, total):
+                for i in range(together):
+                    b = c * together + i
+                    for j in range(2):
+                        mine = ((sel_ref[b, j] == s) & (b > s)).astype(F32)
+                        total = total + arrived[n, b, j].astype(F32) * mine
                 return total
 
-            total = lax.fori_loop(s, blocks, add, jnp.zeros((piece, size), F32))
+            total = lax.fori_loop((s + 1) // together, blocks // together, add, jnp.zeros((piece, size), F32))
             home[n, s] = total.astype(BF16)
 
         send_all(lambda dest: pltpu.make_async_remote_copy(
@@ -214,6 +224,11 @@
                                   ks, vs, kt, vt, dk, dv)
             outv[n, g, span, :] = out
             dqv[n, g, span, :] = dq
+
+        for m in range(1, heads):
+            @pl.when(at == (m - 1) * group)
+            def _(m=m):
+                relay(m)
 
         @pl.when(g == group - 1)
         def _():

time: 108 us -> 99.5 us (0.921)
  Pallas kernels: 94.1 us -> 85.2 us
    pallas_call x1, Pallas kernels: 94.1 us -> 85.2 us  [step(): pl.pallas_call(functools.partial(step_kernel, blocks, halves, tile), in_s...]
where the time goes in v4:
time: 99.5 us; the launch traced here: 99.2 us
  Pallas kernels  85.2 us (86%)
  local copies, waits for them, and re-layouts  11.6 us (12%)
  other arithmetic  1.72 us (2%)
    pallas_call x1, Pallas kernels, step(): pl.pallas_call(functools.partial(step_kernel, blocks, halves, tile), in_s...  85.2 us
    unnamed x13, local copies, waits for them, and re-layouts  6.87 us

profile of v4, /device:TPU:0, one launch (start us, length us, event | category | flops | bytes accessed | tf_op | source)
XLA Modules:
  0.0 99.2 jit_solution(15218034921926550264)
XLA Ops:
  0.6 0.0 copy-start.4
  0.6 0.7 copy-done.4
  1.3 0.7 copy.13.sel_ref
  2.0 1.3 %copy_bitcast_fusion.3 = (bf16[1,512,4,128]{3,1,0,2:T(8,128)(2,1)S(1)}, bf16[1,512,4,128]{3,1,0,2:T(8,128)(2,1)S(1)}) fusion(bf16[512,4,128]{2,1,0:T(4,128)(2,1)} %param.7, bf16[512,4,128]{2,1,0:T(4,128)(2,1)} %param.6), kind=kLoop, calls=%fused_computation.6 | loop fusion | bytes 2097152 | tf_op jit(solution)/shard_map/stack | solution.py:314
  3.3 0.0 copy-start.2
  3.3 0.9 fusion.1.own_ref
  4.2 0.0 copy-start.1
  4.2 0.9 fusion
  5.1 0.0 copy-done.2
  5.1 0.6 copy-done.1
  5.7 1.7 %copy_bitcast_fusion = (bf16[4,2,512,128]{3,2,1,0:T(8,128)(2,1)}, bf16[4,2,512,128]{3,2,1,0:T(8,128)(2,1)}) fusion(bf16[512,2,4,128]{3,2,1,0:T(4,128)(2,1)S(1)} %copy-done.1, bf16[512,2,4,128]{3,2,1,0:T(4,128)(2,1)S(1)} %copy-done.2), kind=kLoop, calls=%fused_computation.2 | loop fusion | bytes 4194304 | tf_op jit(solution)/shard_map/transpose | solution.py:317
  7.4 85.2 %shard_map.84 = (bf16[2,16,64,128]{3,2,1,0:T(8,128)(2,1)}, bf16[4,2,512,128]{3,2,1,0:T(8,128)(2,1)}, bf16[4,2,512,128]{3,2,1,0:T(8,128)(2,1)}) custom-call(s32[16,2]{1,0:T(8,128)} %copy.13.sel_ref, bf16[2,16,64,128]{3,2,1,0:T(8,128)(2,1)} %bitcast.23, bf16[2,2,512,128]{3,2,1,0:T(8,128)(2,1)} %fusion.1.own_ref, ...), custom_call_target="tpu_custom_call" | custom-call | tf_op jit(solution)/shard_map/pallas_call | solution.py:274
  92.6 0.0 copy-start
  92.6 3.1 %copy.15 = bf16[512,2,4,128]{3,2,1,0:T(4,128)(2,1)} copy(bf16[512,2,4,128]{3,0,1,2:T(8,128)(2,1)} %bitcast.25) | data formatting | bytes 2097152
  95.7 0.0 copy-done
  95.7 0.0 copy-start.3
  95.7 1.8 %copy.16 = bf16[512,2,4,128]{3,2,1,0:T(4,128)(2,1)} copy(bf16[512,2,4,128]{3,0,1,2:T(8,128)(2,1)S(1)} %bitcast.24) | data formatting | bytes 2097152
  97.5 0.0 copy-done.3
  97.5 0.5 copy.22
  98.1 1.2 %slice_bitcast_fusion = (bf16[512,2,128]{2,1,0:T(2,128)(2,1)}, bf16[512,2,128]{2,1,0:T(2,128)(2,1)}) fusion(bf16[2,512,2,128]{3,2,1,0:T(2,128)(2,1)S(1)} %bitcast.22), kind=kLoop, calls=%fused_computation.8 | loop fusion | bytes 1048576 | tf_op jit(solution)/shard_map/squeeze | solution.py:320
Async XLA Ops:
  0.6 0.7 copy-start.4
  3.3 1.7 %copy-start.2 = (bf16[512,2,4,128]{3,2,1,0:T(4,128)(2,1)S(1)}, bf16[512,2,4,128]{3,2,1,0:T(4,128)(2,1)}, u32[]{:S(2)}) copy-start(bf16[512,2,4,128]{3,2,1,0:T(4,128)(2,1)} %param.5) | copy-start | bytes 3145732
  4.2 1.5 %copy-start.1 = (bf16[512,2,4,128]{3,2,1,0:T(4,128)(2,1)S(1)}, bf16[512,2,4,128]{3,2,1,0:T(4,128)(2,1)}, u32[]{:S(2)}) copy-start(bf16[512,2,4,128]{3,2,1,0:T(4,128)(2,1)} %param.8) | copy-start | bytes 3145732
  92.6 3.1 %copy-start = (bf16[4,2,512,128]{3,2,1,0:T(8,128)(2,1)S(1)}, bf16[4,2,512,128]{3,2,1,0:T(8,128)(2,1)}, u32[]{:S(2)}) copy-start(bf16[4,2,512,128]{3,2,1,0:T(8,128)(2,1)} %get-tuple-element.8) | copy-start | bytes 3145732
  95.7 1.8 %copy-start.3 = (bf16[2,16,64,128]{3,2,1,0:T(8,128)(2,1)S(1)}, bf16[2,16,64,128]{3,2,1,0:T(8,128)(2,1)}, u32[]{:S(2)}) copy-start(bf16[2,16,64,128]{3,2,1,0:T(8,128)(2,1)} %get-tuple-element.9) | copy-start | bytes 1572868

commit v5 on v4

--- a/solution.py
+++ b/solution.py
@@ -162,11 +162,19 @@
     def collect(n):
         back_first(n).wait_recv()
 
-        @pl.loop(0, blocks)
-        def _(s):
+        def deliver(i):
+            dest = lax.rem(me + i, blocks)
+            pltpu.make_async_remote_copy(
+                home.at[n, dest], ret.at[n, me], b2.at[n], c2.at[n],
+                device_id={"ctx": dest, "head": half}).start()
+
+        @pl.loop(1, blocks + 1)
+        def _(i):
+            s = lax.rem(me + i, blocks)
+
             def add(c, total):
-                for i in range(together):
-                    b = c * together + i
+                for k in range(together):
+                    b = c * together + k
                     for j in range(2):
                         mine = ((sel_ref[b, j] == s) & (b > s)).astype(F32)
                         total = total + arrived[n, b, j].astype(F32) * mine
@@ -175,8 +183,10 @@
             total = lax.fori_loop((s + 1) // together, blocks // together, add, jnp.zeros((piece, size), F32))
             home[n, s] = total.astype(BF16)
 
-        send_all(lambda dest: pltpu.make_async_remote_copy(
-            home.at[n, dest], ret.at[n, me], b2.at[n], c2.at[n], device_id={"ctx": dest, "head": half}))
+            @pl.when(i > 1)
+            def _():
+                deliver(i - 1)
+
         ret[n, me] = home[n, me]
 
     def results(n):

time: 99.5 us -> 98.9 us (level)
  no operation moved by 1% of the time
where the time goes in v5:
time: 98.9 us; the launch traced here: 98.6 us
  Pallas kernels  84.6 us (86%)
  local copies, waits for them, and re-layouts  11.6 us (12%)
  other arithmetic  1.72 us (2%)
    pallas_call x1, Pallas kernels, step(): pl.pallas_call(functools.partial(step_kernel, blocks, halves, tile), in_s...  84.6 us
    unnamed x13, local copies, waits for them, and re-layouts  6.87 us

profile of v5, /device:TPU:0, one launch (start us, length us, event | category | flops | bytes accessed | tf_op | source)
XLA Modules:
  0.0 98.6 jit_solution(6268071317288070542)
XLA Ops:
  0.6 0.0 copy-start.4
  0.6 0.7 copy-done.4
  1.3 0.7 copy.13.sel_ref
  2.0 1.3 %copy_bitcast_fusion.3 = (bf16[1,512,4,128]{3,1,0,2:T(8,128)(2,1)S(1)}, bf16[1,512,4,128]{3,1,0,2:T(8,128)(2,1)S(1)}) fusion(bf16[512,4,128]{2,1,0:T(4,128)(2,1)} %param.7, bf16[512,4,128]{2,1,0:T(4,128)(2,1)} %param.6), kind=kLoop, calls=%fused_computation.6 | loop fusion | bytes 2097152 | tf_op jit(solution)/shard_map/stack | solution.py:324
  3.3 0.0 copy-start.2
  3.3 0.9 fusion.1.own_ref
  4.2 0.0 copy-start.1
  4.2 0.9 fusion
  5.1 0.0 copy-done.2
  5.1 0.6 copy-done.1
  5.7 1.7 %copy_bitcast_fusion = (bf16[4,2,512,128]{3,2,1,0:T(8,128)(2,1)}, bf16[4,2,512,128]{3,2,1,0:T(8,128)(2,1)}) fusion(bf16[512,2,4,128]{3,2,1,0:T(4,128)(2,1)S(1)} %copy-done.1, bf16[512,2,4,128]{3,2,1,0:T(4,128)(2,1)S(1)} %copy-done.2), kind=kLoop, calls=%fused_computation.2 | loop fusion | bytes 4194304 | tf_op jit(solution)/shard_map/transpose | solution.py:327
  7.4 84.6 %shard_map.84 = (bf16[2,16,64,128]{3,2,1,0:T(8,128)(2,1)}, bf16[4,2,512,128]{3,2,1,0:T(8,128)(2,1)}, bf16[4,2,512,128]{3,2,1,0:T(8,128)(2,1)}) custom-call(s32[16,2]{1,0:T(8,128)} %copy.13.sel_ref, bf16[2,16,64,128]{3,2,1,0:T(8,128)(2,1)} %bitcast.23, bf16[2,2,512,128]{3,2,1,0:T(8,128)(2,1)} %fusion.1.own_ref, ...), custom_call_target="tpu_custom_call" | custom-call | tf_op jit(solution)/shard_map/pallas_call | solution.py:284
  92.0 0.0 copy-start
  92.0 3.1 %copy.15 = bf16[512,2,4,128]{3,2,1,0:T(4,128)(2,1)} copy(bf16[512,2,4,128]{3,0,1,2:T(8,128)(2,1)} %bitcast.25) | data formatting | bytes 2097152
  95.1 0.0 copy-done
  95.1 0.0 copy-start.3
  95.1 1.8 %copy.16 = bf16[512,2,4,128]{3,2,1,0:T(4,128)(2,1)} copy(bf16[512,2,4,128]{3,0,1,2:T(8,128)(2,1)S(1)} %bitcast.24) | data formatting | bytes 2097152
  96.9 0.0 copy-done.3
  96.9 0.5 copy.22
  97.5 1.2 %slice_bitcast_fusion = (bf16[512,2,128]{2,1,0:T(2,128)(2,1)}, bf16[512,2,128]{2,1,0:T(2,128)(2,1)}) fusion(bf16[2,512,2,128]{3,2,1,0:T(2,128)(2,1)S(1)} %bitcast.22), kind=kLoop, calls=%fused_computation.8 | loop fusion | bytes 1048576 | tf_op jit(solution)/shard_map/squeeze | solution.py:330
Async XLA Ops:
  0.6 0.7 copy-start.4
  3.3 1.7 %copy-start.2 = (bf16[512,2,4,128]{3,2,1,0:T(4,128)(2,1)S(1)}, bf16[512,2,4,128]{3,2,1,0:T(4,128)(2,1)}, u32[]{:S(2)}) copy-start(bf16[512,2,4,128]{3,2,1,0:T(4,128)(2,1)} %param.5) | copy-start | bytes 3145732
  4.2 1.5 %copy-start.1 = (bf16[512,2,4,128]{3,2,1,0:T(4,128)(2,1)S(1)}, bf16[512,2,4,128]{3,2,1,0:T(4,128)(2,1)}, u32[]{:S(2)}) copy-start(bf16[512,2,4,128]{3,2,1,0:T(4,128)(2,1)} %param.8) | copy-start | bytes 3145732
  92.0 3.1 %copy-start = (bf16[4,2,512,128]{3,2,1,0:T(8,128)(2,1)S(1)}, bf16[4,2,512,128]{3,2,1,0:T(8,128)(2,1)}, u32[]{:S(2)}) copy-start(bf16[4,2,512,128]{3,2,1,0:T(8,128)(2,1)} %get-tuple-element.8) | copy-start | bytes 3145732
  95.1 1.8 %copy-start.3 = (bf16[2,16,64,128]{3,2,1,0:T(8,128)(2,1)S(1)}, bf16[2,16,64,128]{3,2,1,0:T(8,128)(2,1)}, u32[]{:S(2)}) copy-start(bf16[2,16,64,128]{3,2,1,0:T(8,128)(2,1)} %get-tuple-element.9) | copy-start | bytes 1572868
